TPU v7x, 256 devices: a whole 4x4x8 slice. The times are simulated.
256 devices in a mesh: gx: 32 (over z, y), gy: 8 (over x, core).
Axes of the slice: x: 4, y: 4, z: 8, core: 2. Of those that a mesh axis runs over, the one named last changes fastest.
Arguments:
- efield: float32 [3, 512, 256, 128], P(None, 'gx', 'gy'), may hold values from -6 to 6
- hfield: float32 [3, 512, 256, 128], P(None, 'gx', 'gy'), may hold values from -6 to 6
- polar: float32 [3, 512, 256, 128], P(None, 'gx', 'gy'), may hold values from -6 to 6
- material_map: int32 [512, 256, 128], P('gx', 'gy'), may hold values from 0 to 2
- via_index: int32 [512, 256, 128], P('gx', 'gy'), may hold values from 0 to 7
- fill_fraction: float32 [512, 256, 128], P('gx', 'gy'), may hold values from 0 to 1
- permittivity: float32 [3], replicated, may hold values from 1 to 5
- conductivity: float32 [3], replicated, may hold values from 0 to 2
- debye_strength: float32 [3], replicated, may hold values from 0.5 to 3
- relax_time: float32 [3], replicated, may hold values from 0.5 to 5
- conformal: float32 [8, 3], replicated, may hold values from 0.3 to 1
Outputs:
- efield_out: float32 [3, 512, 256, 128], P(None, 'gx', 'gy')
- hfield_out: float32 [3, 512, 256, 128], P(None, 'gx', 'gy')
- polar_out: float32 [3, 512, 256, 128], P(None, 'gx', 'gy')
Inputs may be any that keep to these rules, and one draw needn't show every extreme that they name: `via_index`: a row of the conformal table.
All inputs are finite; a program needn't handle non-finite values.
Results may differ from a plain program's by a relative error of at most 0.00002.
Values sent between devices are 32-bit elements; how exact they have to be, the bound alone decides.
No kernel may reach another device: no remote copies, remote signals or barrier semaphores. Data moves between devices by JAX's collectives and lax.ppermute only.
A program may use at most 64 MiB of HBM per device.

v0:
```python
import jax
import jax.numpy as jnp
from jax import lax
from jax.sharding import PartitionSpec as P

STEPS = 4


time_step = 0.55


def padded(value, sides, width):
    for axis, dim in sides:
        size, length = (lax.axis_size(axis), value.shape[dim])
        up = [(i, (i + 1) % size) for i in range(size - 1)]
        down = [(j, i) for i, j in up]
        last = lax.slice_in_dim(value, length - width, length, axis=dim)
        initial = lax.slice_in_dim(value, 0, width, axis=dim)
        before = lax.ppermute(last, axis, up)
        after = lax.ppermute(initial, axis, down)
        value = jnp.concatenate([before, value, after], axis=dim)
    return value


def passed_along(value, axis, steps):
    count = lax.axis_size(axis)
    initial, last = (max(0, -steps), min(count, count - steps))
    return lax.ppermute(value, axis, [(source, source + steps) for source in range(initial, last)])


def select(ids, table, count):
    total = jnp.zeros(ids.shape, jnp.float32)
    for entry in range(count):
        total = total + jnp.where(ids == entry, table[entry], jnp.zeros((), table.dtype))
    return total


def coefficients(
    material_map,
    via_index,
    fill_fraction,
    permittivity,
    conductivity,
    debye_strength,
    relax_time,
    conformal,
):
    count = permittivity.shape[0]
    eps = select(material_map, permittivity, count) * (1.0 + fill_fraction)
    loss = select(material_map, conductivity, count) * time_step / (2.0 * eps)
    ca_coef = (1.0 - loss) / (1.0 + loss)
    cb_coef = time_step / (eps * (1.0 + loss))
    cbp_coef = cb_coef / time_step
    relax = select(material_map, relax_time, count)
    kp_coef = (2.0 * relax - time_step) / (2.0 * relax + time_step)
    bp_coef = (
        2.0 * time_step * select(material_map, debye_strength, count) / (2.0 * relax + time_step)
    )
    vias = conformal.shape[0]
    weights = [cb_coef * select(via_index, conformal[:, comp], vias) for comp in range(3)]
    return jnp.stack([ca_coef, cbp_coef, kp_coef, bp_coef] + weights)


def forward(field, axis, plane):
    rest = lax.slice_in_dim(field, 1, field.shape[axis], axis=axis)
    return jnp.concatenate([rest, plane], axis=axis)


def backward(field, axis, plane):
    rest = lax.slice_in_dim(field, 0, field.shape[axis] - 1, axis=axis)
    return jnp.concatenate([plane, rest], axis=axis)


def curl_e(efield, y_next, x_next):
    ex_comp, ey_comp, ez_comp = (efield[0], efield[1], efield[2])
    z_plane = jnp.zeros_like(ex_comp[:, :, :1])
    cx_part = forward(ez_comp, 1, y_next[1]) - ez_comp - (forward(ey_comp, 2, z_plane) - ey_comp)
    cy_part = forward(ex_comp, 2, z_plane) - ex_comp - (forward(ez_comp, 0, x_next[1]) - ez_comp)
    cz_part = forward(ey_comp, 0, x_next[0]) - ey_comp - (forward(ex_comp, 1, y_next[0]) - ex_comp)
    return jnp.stack([cx_part, cy_part, cz_part])


def curl_h(hfield, y_prev, x_prev):
    hx_comp, hy_comp, hz_comp = (hfield[0], hfield[1], hfield[2])
    z_plane = jnp.zeros_like(hx_comp[:, :, :1])
    cx_part = hz_comp - backward(hz_comp, 1, y_prev[1]) - (hy_comp - backward(hy_comp, 2, z_plane))
    cy_part = hx_comp - backward(hx_comp, 2, z_plane) - (hz_comp - backward(hz_comp, 0, x_prev[1]))
    cz_part = (
        hy_comp - backward(hy_comp, 0, x_prev[0]) - (hx_comp - backward(hx_comp, 1, y_prev[0]))
    )
    return jnp.stack([cx_part, cy_part, cz_part])


def inside_range(count, position, devices):
    global_pos = jnp.arange(count + 8) + position * count - 4
    return ((global_pos >= 0) & (global_pos < count * devices)).astype(jnp.float32)


def cell_stack(efield, hfield, polar, coef):
    return jnp.concatenate([efield, hfield, polar, coef], 0)


def rim_coefs(widened):
    return widened[9:16]


def shards(
    efield,
    hfield,
    polar,
    material_map,
    via_index,
    fill_fraction,
    permittivity,
    conductivity,
    debye_strength,
    relax_time,
    conformal,
):
    depth = efield.shape[1]
    coef = coefficients(
        material_map,
        via_index,
        fill_fraction,
        permittivity,
        conductivity,
        debye_strength,
        relax_time,
        conformal,
    )
    stacked = cell_stack(efield, hfield, polar, coef)
    widened = padded(stacked, (("gx", 1),), 4)
    inside = inside_range(depth, lax.axis_index("gx"), lax.axis_size("gx"))[:, None, None]
    elec, magn, pol = (widened[0:3], widened[3:6], widened[6:9])
    coef = rim_coefs(widened)
    x_zero = jnp.zeros((2, 1) + elec.shape[2:], jnp.float32)
    for step in range(STEPS):
        y_next = passed_along(jnp.stack([elec[0][:, :1], elec[2][:, :1]]), "gy", -1)
        magn = magn - time_step * curl_e(elec, y_next, x_zero)
        magn = magn * inside
        y_prev = passed_along(jnp.stack([magn[0][:, -1:], magn[2][:, -1:]]), "gy", 1)
        pol_new = coef[2] * pol + coef[3] * elec
        elec = coef[0] * elec + coef[4:7] * curl_h(magn, y_prev, x_zero) - coef[1] * (pol_new - pol)
        pol = pol_new
    elec = elec[:, 4 : 4 + depth]
    magn = magn[:, 4 : 4 + depth]
    pol = pol[:, 4 : 4 + depth]
    return (elec, magn, pol)


def solution(mesh):
    placed = (
        P(None, "gx", "gy", None),
        P(None, "gx", "gy", None),
        P(None, "gx", "gy", None),
        P("gx", "gy", None),
        P("gx", "gy", None),
        P("gx", "gy", None),
        P(),
        P(),
        P(),
        P(),
        P(),
    )
    return jax.shard_map(
        shards,
        mesh=mesh,
        in_specs=placed,
        out_specs=(P(None, "gx", "gy", None), P(None, "gx", "gy", None), P(None, "gx", "gy", None)),
        check_vma=False,
    )
```

profile of v0, /device:TPU:122, one launch (start us, length us, event | category | flops | bytes accessed | tf_op | source)
XLA Modules:
  0.0 141.0 jit_solution(12992325127451088842)
XLA Ops:
  0.7 2.1 %fusion.58 = (f32[1,1]{0,1:T(1,128)}, f32[1,1]{0,1:T(1,128)}, f32[1,1]{0,1:T(1,128)}, f32[1,1]{0,1:T(1,128)}, f32[1,1]{0,1:T(1,128)}, /*index=5*/f32[1,1]{0,1:T(...) fusion(f32[8,3]{0,1:T(4,128)} %param.21), kind=kLoop, calls=%fused_computation.203 | loop fusion | bytes 152 | tf_op jit(solution)/shard_map/slice | solution.py:34
  2.8 1.5 %fusion.59 = (f32[1,1]{0,1:T(1,128)}, f32[1,1]{0,1:T(1,128)}, f32[1,1]{0,1:T(1,128)}, f32[1,1]{0,1:T(1,128)}, f32[1,1]{0,1:T(1,128)}) fusion(f32[8,3]{0,1:T(4,128)} %param.21), kind=kLoop, calls=%fused_computation.204 | loop fusion | bytes 40 | tf_op jit(solution)/shard_map/slice | solution.py:34
  4.3 1.4 %fusion.62 = (f32[1]{0:T(128)}, f32[1]{0:T(128)}, f32[1]{0:T(128)}) fusion(f32[3]{0:T(128)} %param.18), kind=kLoop, calls=%fused_computation.207 | loop fusion | bytes 24 | tf_op jit(solution)/shard_map/slice | solution.py:34
  5.7 1.4 fusion.63
  7.1 1.2 constant_dynamic-update-slice_fusion.2
  8.3 0.7 fusion.61
  8.9 0.7 fusion.60
  9.7 0.9 copy-done.2
  10.7 4.1 %bitcast_dynamic-update-slice_fusion.6 = (f32[16,16,32,128]{3,2,1,0:T(8,128)S(1)}, pred[16,32,128]{2,1,0:T(8,128)(4,1)S(1)}, pred[16,32,128]{2,1,0:T(8,128)(4,1)S(1)}, pred[16,32,128]{2,1,0:T(8,128)(4,1)S(1)}) fusion(f32[16,16,32,128]{3,2,1,0:T(8,128)S(1)} %constant_dynamic-update-slice_fusion, f32[16,32,128]{2,1,0:T(8,128)S(1)} %copy-done.2, f32[]{:T(128)} %bitcast.5, ...), kind=kLoop, calls=%fused_computation.154 | loop fusion | flops 1376256 | bytes 983064
  14.8 4.0 %bitcast_dynamic-update-slice_fusion.5 = f32[16,16,32,128]{3,2,1,0:T(8,128)S(1)} fusion(f32[16,16,32,128]{3,2,1,0:T(8,128)S(1)} %get-tuple-element.23, pred[16,32,128]{2,1,0:T(8,128)(4,1)S(1)} %get-tuple-element.26, f32[]{:T(128)} %bitcast.2, pred[16,32,128]{2,1,0:T(8,128)(4,1)S(1)} %get-tuple-element.25, f32[]{:T(128)} %bitcast.1, ...), kind=kLoop, calls=%fused_computation.153 | loop fusion | flops 1245184 | bytes 720920
  18.8 2.0 %bitcast_dynamic-update-slice_fusion.4 = f32[16,16,32,128]{3,2,1,0:T(8,128)S(1)} fusion(f32[16,16,32,128]{3,2,1,0:T(8,128)S(1)} %bitcast_dynamic-update-slice_fusion.5, pred[16,32,128]{2,1,0:T(8,128)(4,1)S(1)} %get-tuple-element.26, pred[16,32,128]{2,1,0:T(8,128)(4,1)S(1)} %get-tuple-element.25, pred[16,32,128]{2,1,0:T(8,128)(4,1)S(1)} %get-tuple-element.24, ...), kind=kLoop, calls=%fused_computation.152 | loop fusion | flops 589824 | bytes 458764
  20.9 3.9 %bitcast_dynamic-update-slice_fusion.3 = f32[16,16,32,128]{3,2,1,0:T(8,128)S(1)} fusion(f32[16,16,32,128]{3,2,1,0:T(8,128)S(1)} %bitcast_dynamic-update-slice_fusion.4, pred[16,32,128]{2,1,0:T(8,128)(4,1)S(1)} %get-tuple-element.26, pred[16,32,128]{2,1,0:T(8,128)(4,1)S(1)} %get-tuple-element.25, pred[16,32,128]{2,1,0:T(8,128)(4,1)S(1)} %get-tuple-element.24, ...), kind=kLoop, calls=%fused_computation.151 | loop fusion | flops 917504 | bytes 458776
  24.8 9.3 %bitcast_dynamic-update-slice_fusion.2 = (f32[16,16,32,128]{3,2,1,0:T(8,128)S(1)}, pred[16,32,128]{2,1,0:T(8,128)(4,1)S(1)}, pred[16,32,128]{2,1,0:T(8,128)(4,1)...) fusion(f32[16,16,32,128]{3,2,1,0:T(8,128)S(1)} %bitcast_dynamic, ...), kind=kLoop, calls=%fused_computation.150 | loop fusion | flops 2752512 | bytes 1507384
  34.1 9.3 %bitcast_dynamic-update-slice_fusion.1 = f32[16,16,32,128]{3,2,1,0:T(8,128)S(1)} fusion(f32[16,16,32,128]{3,2,1,0:T(8,128)S(1)} %get-tuple-element.14, pred[16,32,128]{2,1,0:T(8,128)(4,1)S(1)} %get-tuple-element.22, pred[16,32,128]{2,1,0:T(8,128)(4,1)S(1)} %get-tuple-element.21, pred[16,32,128]{2,1,0:T(8,128)(4,1)S(1)} %get-tuple-element.20, ...), kind=kLoop, calls=%fused_computation.149 | loop fusion | flops 2228224 | bytes 1245240
  43.5 9.3 %bitcast_dynamic-update-slice_fusion = f32[16,16,32,128]{3,2,1,0:T(8,128)S(1)} fusion(f32[16,16,32,128]{3,2,1,0:T(8,128)S(1)} %bitcast_dynamic-update-slice_fusion.1, pred[16,32,128]{2,1,0:T(8,128)(4,1)S(1)} %get-tuple-element.22, pred[16,32,128]{2,1,0:T(8,128)(4,1)S(1)} %get-tuple-element.21, pred[16,32,128]{2,1,0:T(8,128)(4,1)S(1)} %get-tuple-element.20, ...), kind=kLoop, calls=%fused_computation.148 | loop fusion | flops 2228224 | bytes 1245240 | tf_op jit(solution)/shard_map/concatenate | solution.py:100
  52.8 1.4 fusion.49
  54.1 0.9 copy-done
  55.1 4.7 %collective-permute-start = (f32[16,4,32,128]{3,2,1,0:T(8,128)}, f32[16,4,32,128]{3,2,1,0:T(8,128)S(1)}, u32[]{:S(2)}, u32[]{:S(2)}) collective-permute-start(f32[16,4,32,128]{3,2,1,0:T(8,128)} %get-tuple-element.35), channel_id=1, source_target_pairs={{0,8},{8,16},{16,24},{24,32},{32,40},{40,48},{48,56},{56,64},{64,7... | collective-permute-start | bytes 3145736 | tf_op jit(solution)/shard_map/ppermute | solution.py:19
  59.8 1.9 %collective-permute-start.1 = (f32[16,4,32,128]{3,2,1,0:T(8,128)S(1)}, f32[16,4,32,128]{3,2,1,0:T(8,128)S(1)}, u32[]{:S(2)}, u32[]{:S(2)}) collective-permute-start(f32[16,4,32,128]{3,2,1,0:T(8,128)S(1)} %get-tuple-element.36), channel_id=1, source_target_pairs={{8,0},{16,8},{24,16},{32,24},{40,32},{48,40},{56,48},{64,56},{72,6... | collective-permute-start | bytes 3145736 | tf_op jit(solution)/shard_map/ppermute | solution.py:20
  61.7 20.8 %collective-permute-done = f32[16,4,32,128]{3,2,1,0:T(8,128)S(1)} collective-permute-done((f32[16,4,32,128]{3,2,1,0:T(8,128)}, f32[16,4,32,128]{3,2,1,0:T(8,128)S(1)}, u32[]{:S(2)}, u32[]{:S(2)}) %collective-permute-start) | collective-permute-done | bytes 1048608 | tf_op jit(solution)/shard_map/ppermute | solution.py:19
  82.5 7.1 %collective-permute-done.1 = f32[16,4,32,128]{3,2,1,0:T(8,128)S(1)} collective-permute-done((f32[16,4,32,128]{3,2,1,0:T(8,128)S(1)}, f32[16,4,32,128]{3,2,1,0:T(8,128)S(1)}, u32[]{:S(2)}, u32[]{:S(2)}) %collective-permute-start.1) | collective-permute-done | bytes 1048608 | tf_op jit(solution)/shard_map/ppermute | solution.py:20
  89.6 1.6 %maximum_bitcast_fusion.5 = (f32[24,32,128]{2,1,0:T(8,128)S(1)}, f32[24,32,128]{2,1,0:T(8,128)S(1)}, f32[24,32,128]{2,1,0:T(8,128)S(1)}, f32[24,32,128]{2,1,0:T(8,128)S(1)}, f32[1,24,32,128]{3,2,1,0:T(8,128)S(1)}) fusion(f32[16,4,32,128]{3,2,1,0:T(8,128)S(1)} %collective-permute-done.1, f32[16,16,32,128]{3,2,1,0:T(8,128)} %copy-done, ...), kind=kLoop, calls=%fused_computation.57 | loop fusion | flops 983040 | bytes 8257536 | tf_op jit(solution)/shard_map/mul | solution.py:143
  91.6 0.2 pad_subtract_fusion.5
  91.8 0.3 copy-done.1
  92.4 1.9 %collective-permute-start.2 = (f32[2,24,1,128]{3,1,2,0:T(8,128)S(1)}, f32[2,24,1,128]{3,1,2,0:T(8,128)S(1)}, u32[]{:S(2)}, u32[]{:S(2)}) collective-permute-start(f32[2,24,1,128]{3,1,2,0:T(8,128)S(1)} %pad_maximum_fusion.5), channel_id=1, source_target_pairs={{1,0},{2,1},{3,2},{4,3},{5,4},{6,5},{7,6},{9,8},{10,9},{11,10},{12... | collective-permute-start | bytes 73736 | tf_op jit(solution)/shard_map/ppermute | solution.py:28
  94.3 0.9 pad_maximum_fusion
  95.4 0.4 collective-permute-done.2
  95.8 0.2 maximum_subtract_fusion.1
  96.9 0.2 copy.129
  97.2 3.5 %collective-permute-start.3 = (f32[2,24,1,128]{3,1,2,0:T(8,128)S(1)}, f32[2,24,1,128]{3,1,2,0:T(8,128)S(1)}, u32[]{:S(2)}, u32[]{:S(2)}) collective-permute-start(f32[2,24,1,128]{3,1,2,0:T(8,128)S(1)} %pad_maximum_fusion.6), channel_id=1, source_target_pairs={{0,1},{1,2},{2,3},{3,4},{4,5},{5,6},{6,7},{8,9},{9,10},{10,11},{11... | collective-permute-start | bytes 73736 | tf_op jit(solution)/shard_map/ppermute | solution.py:28
  100.8 1.5 %collective-permute-done.3 = f32[2,24,1,128]{3,1,2,0:T(8,128)S(1)} collective-permute-done((f32[2,24,1,128]{3,1,2,0:T(8,128)S(1)}, f32[2,24,1,128]{3,1,2,0:T(8,128)S(1)}, u32[]{:S(2)}, u32[]{:S(2)}) %collective-permute-start.3) | collective-permute-done | bytes 24608 | tf_op jit(solution)/shard_map/ppermute | solution.py:28
  102.3 0.3 pad_subtract_fusion.4
  102.6 0.4 fusion.19
  103.0 0.8 fusion.2
  104.2 1.9 %collective-permute-start.4 = (f32[2,24,1,128]{3,1,2,0:T(8,128)S(1)}, f32[2,24,1,128]{3,1,2,0:T(8,128)S(1)}, u32[]{:S(2)}, u32[]{:S(2)}) collective-permute-start(f32[2,24,1,128]{3,1,2,0:T(8,128)S(1)} %pad_maximum_fusion.7), channel_id=1, source_target_pairs={{1,0},{2,1},{3,2},{4,3},{5,4},{6,5},{7,6},{9,8},{10,9},{11,10},{12... | collective-permute-start | bytes 73736 | tf_op jit(solution)/shard_map/ppermute | solution.py:28
  106.6 1.0 collective-permute-done.4
  107.7 0.3 pad_subtract_fusion.3
  107.9 0.4 fusion.21
  108.4 0.5 fusion.4
  108.9 0.2 copy.127
  109.2 3.7 %collective-permute-start.5 = (f32[2,24,1,128]{3,1,2,0:T(8,128)S(1)}, f32[2,24,1,128]{3,1,2,0:T(8,128)S(1)}, u32[]{:S(2)}, u32[]{:S(2)}) collective-permute-start(f32[2,24,1,128]{3,1,2,0:T(8,128)S(1)} %pad_maximum_fusion.8), channel_id=1, source_target_pairs={{0,1},{1,2},{2,3},{3,4},{4,5},{5,6},{6,7},{8,9},{9,10},{10,11},{11... | collective-permute-start | bytes 73736 | tf_op jit(solution)/shard_map/ppermute | solution.py:28
  113.0 1.4 collective-permute-done.5
  114.4 0.3 pad_subtract_fusion.2
  114.7 0.4 fusion.23
  115.1 0.9 fusion.6
  116.4 1.9 %collective-permute-start.6 = (f32[2,24,1,128]{3,1,2,0:T(8,128)S(1)}, f32[2,24,1,128]{3,1,2,0:T(8,128)S(1)}, u32[]{:S(2)}, u32[]{:S(2)}) collective-permute-start(f32[2,24,1,128]{3,1,2,0:T(8,128)S(1)} %pad_maximum_fusion.9), channel_id=1, source_target_pairs={{1,0},{2,1},{3,2},{4,3},{5,4},{6,5},{7,6},{9,8},{10,9},{11,10},{12... | collective-permute-start | bytes 73736 | tf_op jit(solution)/shard_map/ppermute | solution.py:28
  118.8 1.0 collective-permute-done.6
  119.8 0.3 pad_subtract_fusion.1
  120.1 0.4 fusion.25
  120.5 0.7 fusion.8
  121.3 3.5 %collective-permute-start.7 = (f32[2,24,1,128]{3,1,2,0:T(8,128)S(1)}, f32[2,24,1,128]{3,1,2,0:T(8,128)S(1)}, u32[]{:S(2)}, u32[]{:S(2)}) collective-permute-start(f32[2,24,1,128]{3,1,2,0:T(8,128)S(1)} %pad_maximum_fusion.10), channel_id=1, source_target_pairs={{0,1},{1,2},{2,3},{3,4},{4,5},{5,6},{6,7},{8,9},{9,10},{10,11},{11... | collective-permute-start | bytes 73736 | tf_op jit(solution)/shard_map/ppermute | solution.py:28
  124.9 1.6 %collective-permute-done.7 = f32[2,24,1,128]{3,1,2,0:T(8,128)S(1)} collective-permute-done((f32[2,24,1,128]{3,1,2,0:T(8,128)S(1)}, f32[2,24,1,128]{3,1,2,0:T(8,128)S(1)}, u32[]{:S(2)}, u32[]{:S(2)}) %collective-permute-start.7) | collective-permute-done | bytes 24608 | tf_op jit(solution)/shard_map/ppermute | solution.py:28
  126.5 0.5 fusion.27
  127.0 1.2 multiply_add_fusion
  128.6 1.9 %collective-permute-start.8 = (f32[2,24,1,128]{3,1,2,0:T(8,128)S(1)}, f32[2,24,1,128]{3,1,2,0:T(8,128)S(1)}, u32[]{:S(2)}, u32[]{:S(2)}) collective-permute-start(f32[2,24,1,128]{3,1,2,0:T(8,128)S(1)} %pad_maximum_fusion.11), channel_id=1, source_target_pairs={{1,0},{2,1},{3,2},{4,3},{5,4},{6,5},{7,6},{9,8},{10,9},{11,10},{12... | collective-permute-start | bytes 73736 | tf_op jit(solution)/shard_map/ppermute | solution.py:28
  131.0 1.0 collective-permute-done.8
  132.0 0.3 pad_subtract_fusion
  132.3 0.4 fusion.31
  132.7 0.8 fusion.12
  133.7 3.5 %collective-permute-start.9 = (f32[2,24,1,128]{3,1,2,0:T(8,128)S(1)}, f32[2,24,1,128]{3,1,2,0:T(8,128)S(1)}, u32[]{:S(2)}, u32[]{:S(2)}) collective-permute-start(f32[2,24,1,128]{3,1,2,0:T(8,128)S(1)} %pad_maximum_fusion.12), channel_id=1, source_target_pairs={{0,1},{1,2},{2,3},{3,4},{4,5},{5,6},{6,7},{8,9},{9,10},{10,11},{11... | collective-permute-start | bytes 73736 | tf_op jit(solution)/shard_map/ppermute | solution.py:28
  137.2 0.9 slice.893
  138.2 0.6 collective-permute-done.9
  138.8 0.5 fusion.33
  139.4 1.7 %fusion.14 = (f32[3,16,32,128]{3,2,1,0:T(8,128)}, f32[3,16,32,128]{3,2,1,0:T(8,128)}) fusion(f32[3,24,32,128]{3,2,1,0:T(8,128)S(1)} %get-tuple-element.7, f32[3,24,32,128]{3,2,1,0:T(8,128)S(1)} %get-tuple-element.27, f32[3,24,32,128]{3,2,1,0:T(8,128)S(1)} %get-tuple-element.6, f32[1,24,32,128]{3,2,1,0:T(8,128)S(1)} %get-tuple-element.38, ...), kind=kLoop, calls=%fused_computation.29 | loop fusion | flops 1572864 | bytes 6422528 | tf_op jit(solution)/shard_map/sub | solution.py:143
  (93 shorter events, 4.7 us)
Async XLA Ops:
  0.6 7.6 %copy-start.7 = (f32[3]{0:T(128)S(1)}, f32[3]{0:T(128)}, u32[]{:S(2)}) copy-start(f32[3]{0:T(128)} %param.20) | copy-start | bytes 40
  0.6 8.3 %copy-start.8 = (f32[3]{0:T(128)S(1)}, f32[3]{0:T(128)}, u32[]{:S(2)}) copy-start(f32[3]{0:T(128)} %param.19) | copy-start | bytes 40
  0.7 8.9 %copy-start.3 = (f32[3,16,32,128]{3,2,1,0:T(8,128)S(1)}, f32[3,16,32,128]{3,2,1,0:T(8,128)}, u32[]{:S(2)}) copy-start(f32[3,16,32,128]{3,2,1,0:T(8,128)} %param.12) | copy-start | bytes 2359300
  8.3 1.4 copy-start.4
  9.7 1.0 copy-start.2
  9.7 1.0 copy-start.5
  10.7 14.1 %copy-start.6 = (s32[16,32,128]{2,1,0:T(8,128)S(1)}, s32[16,32,128]{2,1,0:T(8,128)}, u32[]{:S(2)}) copy-start(s32[16,32,128]{2,1,0:T(8,128)} %param.15) | copy-start | bytes 786436
  52.7 2.3 %copy-start = (f32[16,16,32,128]{3,2,1,0:T(8,128)}, f32[16,16,32,128]{3,2,1,0:T(8,128)S(1)}, u32[]{:S(2)}) copy-start(f32[16,16,32,128]{3,2,1,0:T(8,128)S(1)} %bitcast_dynamic-update-slice_fusion) | copy-start | bytes 12582916
  55.1 27.4 %collective-permute-start = (f32[16,4,32,128]{3,2,1,0:T(8,128)}, f32[16,4,32,128]{3,2,1,0:T(8,128)S(1)}, u32[]{:S(2)}, u32[]{:S(2)}) collective-permute-start(f32[16,4,32,128]{3,2,1,0:T(8,128)} %get-tuple-element.35), channel_id=1, source_target_pairs={{0,8},{8,16},{16,24},{24,32},{32,40},{40,48},{48,56},{56,64},{64,7... | collective-permute-start | bytes 3145736 | tf_op jit(solution)/shard_map/ppermute | solution.py:19
  59.8 29.8 %collective-permute-start.1 = (f32[16,4,32,128]{3,2,1,0:T(8,128)S(1)}, f32[16,4,32,128]{3,2,1,0:T(8,128)S(1)}, u32[]{:S(2)}, u32[]{:S(2)}) collective-permute-start(f32[16,4,32,128]{3,2,1,0:T(8,128)S(1)} %get-tuple-element.36), channel_id=1, source_target_pairs={{8,0},{16,8},{24,16},{32,24},{40,32},{48,40},{56,48},{64,56},{72,6... | collective-permute-start | bytes 3145736 | tf_op jit(solution)/shard_map/ppermute | solution.py:20
  89.6 2.6 %copy-start.1 = (f32[16,16,32,128]{3,2,1,0:T(8,128)S(1)}, f32[16,16,32,128]{3,2,1,0:T(8,128)}, u32[]{:S(2)}) copy-start(f32[16,16,32,128]{3,2,1,0:T(8,128)} %copy-done) | copy-start | bytes 12582916
  92.4 3.4 %collective-permute-start.2 = (f32[2,24,1,128]{3,1,2,0:T(8,128)S(1)}, f32[2,24,1,128]{3,1,2,0:T(8,128)S(1)}, u32[]{:S(2)}, u32[]{:S(2)}) collective-permute-start(f32[2,24,1,128]{3,1,2,0:T(8,128)S(1)} %pad_maximum_fusion.5), channel_id=1, source_target_pairs={{1,0},{2,1},{3,2},{4,3},{5,4},{6,5},{7,6},{9,8},{10,9},{11,10},{12... | collective-permute-start | bytes 73736 | tf_op jit(solution)/shard_map/ppermute | solution.py:28
  97.2 5.1 %collective-permute-start.3 = (f32[2,24,1,128]{3,1,2,0:T(8,128)S(1)}, f32[2,24,1,128]{3,1,2,0:T(8,128)S(1)}, u32[]{:S(2)}, u32[]{:S(2)}) collective-permute-start(f32[2,24,1,128]{3,1,2,0:T(8,128)S(1)} %pad_maximum_fusion.6), channel_id=1, source_target_pairs={{0,1},{1,2},{2,3},{3,4},{4,5},{5,6},{6,7},{8,9},{9,10},{10,11},{11... | collective-permute-start | bytes 73736 | tf_op jit(solution)/shard_map/ppermute | solution.py:28
  104.2 3.4 %collective-permute-start.4 = (f32[2,24,1,128]{3,1,2,0:T(8,128)S(1)}, f32[2,24,1,128]{3,1,2,0:T(8,128)S(1)}, u32[]{:S(2)}, u32[]{:S(2)}) collective-permute-start(f32[2,24,1,128]{3,1,2,0:T(8,128)S(1)} %pad_maximum_fusion.7), channel_id=1, source_target_pairs={{1,0},{2,1},{3,2},{4,3},{5,4},{6,5},{7,6},{9,8},{10,9},{11,10},{12... | collective-permute-start | bytes 73736 | tf_op jit(solution)/shard_map/ppermute | solution.py:28
  109.2 5.1 %collective-permute-start.5 = (f32[2,24,1,128]{3,1,2,0:T(8,128)S(1)}, f32[2,24,1,128]{3,1,2,0:T(8,128)S(1)}, u32[]{:S(2)}, u32[]{:S(2)}) collective-permute-start(f32[2,24,1,128]{3,1,2,0:T(8,128)S(1)} %pad_maximum_fusion.8), channel_id=1, source_target_pairs={{0,1},{1,2},{2,3},{3,4},{4,5},{5,6},{6,7},{8,9},{9,10},{10,11},{11... | collective-permute-start | bytes 73736 | tf_op jit(solution)/shard_map/ppermute | solution.py:28
  116.4 3.4 %collective-permute-start.6 = (f32[2,24,1,128]{3,1,2,0:T(8,128)S(1)}, f32[2,24,1,128]{3,1,2,0:T(8,128)S(1)}, u32[]{:S(2)}, u32[]{:S(2)}) collective-permute-start(f32[2,24,1,128]{3,1,2,0:T(8,128)S(1)} %pad_maximum_fusion.9), channel_id=1, source_target_pairs={{1,0},{2,1},{3,2},{4,3},{5,4},{6,5},{7,6},{9,8},{10,9},{11,10},{12... | collective-permute-start | bytes 73736 | tf_op jit(solution)/shard_map/ppermute | solution.py:28
  121.3 5.1 %collective-permute-start.7 = (f32[2,24,1,128]{3,1,2,0:T(8,128)S(1)}, f32[2,24,1,128]{3,1,2,0:T(8,128)S(1)}, u32[]{:S(2)}, u32[]{:S(2)}) collective-permute-start(f32[2,24,1,128]{3,1,2,0:T(8,128)S(1)} %pad_maximum_fusion.10), channel_id=1, source_target_pairs={{0,1},{1,2},{2,3},{3,4},{4,5},{5,6},{6,7},{8,9},{9,10},{10,11},{11... | collective-permute-start | bytes 73736 | tf_op jit(solution)/shard_map/ppermute | solution.py:28
  128.6 3.4 %collective-permute-start.8 = (f32[2,24,1,128]{3,1,2,0:T(8,128)S(1)}, f32[2,24,1,128]{3,1,2,0:T(8,128)S(1)}, u32[]{:S(2)}, u32[]{:S(2)}) collective-permute-start(f32[2,24,1,128]{3,1,2,0:T(8,128)S(1)} %pad_maximum_fusion.11), channel_id=1, source_target_pairs={{1,0},{2,1},{3,2},{4,3},{5,4},{6,5},{7,6},{9,8},{10,9},{11,10},{12... | collective-permute-start | bytes 73736 | tf_op jit(solution)/shard_map/ppermute | solution.py:28
  133.7 5.1 %collective-permute-start.9 = (f32[2,24,1,128]{3,1,2,0:T(8,128)S(1)}, f32[2,24,1,128]{3,1,2,0:T(8,128)S(1)}, u32[]{:S(2)}, u32[]{:S(2)}) collective-permute-start(f32[2,24,1,128]{3,1,2,0:T(8,128)S(1)} %pad_maximum_fusion.12), channel_id=1, source_target_pairs={{0,1},{1,2},{2,3},{3,4},{4,5},{5,6},{6,7},{8,9},{9,10},{10,11},{11... | collective-permute-start | bytes 73736 | tf_op jit(solution)/shard_map/ppermute | solution.py:28
where the time goes:
time: 142 us; the launch traced here: 141 us
  other arithmetic  56.8 us (40%)
  waiting for transfers between devices  36.5 us (26%)
  starting transfers between devices  28.5 us (20%)
  local copies, waits for them, and re-layouts  17.7 us (12%)
  between operations  1.47 us (1%)
    unnamed x6, other arithmetic  32.7 us
    ppermute x8, starting transfers between devices, passed_along(): lax.ppermute(value, axis, [(source, source + steps) for source in range(i...  21.9 us
    ppermute x1, waiting for transfers between devices, padded(): before = lax.ppermute(last, axis, up)  20.8 us
    concatenate x1, other arithmetic, cell_stack(): return jnp.concatenate([efield, hfield, polar, coef], 0)  9.29 us
    ppermute x8, waiting for transfers between devices, passed_along(): lax.ppermute(value, axis, [(source, source + steps) for source in range(i...  8.66 us
    slice x6, local copies, waits for them, and re-layouts, select(): table[entry]  7.71 us
    ppermute x1, waiting for transfers between devices, padded(): after = lax.ppermute(initial, axis, down)  7.12 us
    unnamed x27, local copies, waits for them, and re-layouts  4.93 us
  transfers between devices with their start and end apart: 10, of which 10 were waited for; matrix products, arithmetic and copies ran while one was open for 2% of the time, Pallas kernels for 0%

commit v1 on v0

v1 whole, which is shorter than its diff:
```python
import jax
import jax.numpy as jnp
from jax import lax
from jax.experimental import pallas as pl
from jax.experimental.pallas import tpu as pltpu
from jax.sharding import PartitionSpec as P

STEPS = 4
DT = 0.55
HALO = 4
F32 = jnp.float32

NXL, NYL, NZ = 16, 32, 128
NXE, NYE = NXL + 2 * HALO, NYL + 8

NMSG = 41


def swapped(value, axis, first):
    size = lax.axis_size(axis)
    pairs = []
    for low in range(first, size - 1, 2):
        pairs += [(low, low + 1), (low + 1, low)]
    return lax.ppermute(value, axis, pairs)


def plane_parts():
    parts = [("e", c, 4, 4 * c) for c in range(3)]
    parts += [("h", 1, 4, 12), ("h", 2, 4, 16), ("h", 0, 3, 20)]
    parts += [("p", c, 3, 23 + 3 * c) for c in range(3)]
    parts += [("c", c, 3, 32 + 3 * c) for c in range(3)]
    return parts


def pack_gx(e, h, p, mat, via, fill, out_a, out_b, ints, sems):
    parity = lax.axis_index("gx") % 2
    src = {"e": e, "h": h, "p": p}
    copies = []
    for which, out in enumerate((out_a, out_b)):
        upward = parity == which
        s4 = jnp.where(upward, NXL - 4, 0)
        s3 = jnp.where(upward, NXL - 3, 0)
        for name, c, n, at in plane_parts():
            s = s4 if n == 4 else s3
            if name == "c":
                ref = (mat, via, fill)[c].at[pl.ds(s, n)]
                dst = out.at[pl.ds(at, n)] if c == 2 else ints.at[which, c]
            else:
                ref = src[name].at[c, pl.ds(s, n)]
                dst = out.at[pl.ds(at, n)]
            copies.append(pltpu.make_async_copy(ref, dst, sems.at[len(copies)]))
    for copy in copies:
        copy.start()
    for copy in copies:
        copy.wait()
    for which, out in enumerate((out_a, out_b)):
        out[32:35] = ints[which, 0].astype(F32)
        out[35:38] = ints[which, 1].astype(F32)


def row_ids():
    return lax.broadcasted_iota(jnp.int32, (8, NZ), 0)


def pack_gy(e, h, p, mat, via, fill, out_c, out_d, rows, irows, sems):
    parity = lax.axis_index("gy") % 2
    copies = []
    for which in range(2):
        upward = parity == which
        r = pl.multiple_of(jnp.where(upward, NYL - 8, 0), 8)
        for k, ref in enumerate((e, h, p)):
            copies.append((ref.at[:, :, pl.ds(r, 8)], rows.at[which, pl.ds(3 * k, 3)]))
        copies.append((fill.at[:, pl.ds(r, 8)], rows.at[which, 9]))
        copies.append((mat.at[:, pl.ds(r, 8)], irows.at[which, 0]))
        copies.append((via.at[:, pl.ds(r, 8)], irows.at[which, 1]))
    copies = [pltpu.make_async_copy(a, b, sems.at[i]) for i, (a, b) in enumerate(copies)]
    for copy in copies:
        copy.start()
    for copy in copies:
        copy.wait()
    low = row_ids() < 4
    for which, out in enumerate((out_c, out_d)):
        upward = parity == which

        def body(x, _):
            tiles = [rows[which, k, x] for k in range(10)]
            tiles += [irows[which, k, x].astype(F32) for k in range(2)]
            for k in range(6):
                a, b = tiles[2 * k], tiles[2 * k + 1]
                up = jnp.where(low, pltpu.roll(a, 4, 0), b)
                down = jnp.where(low, a, pltpu.roll(b, 4, 0))
                out[k, x] = jnp.where(upward, up, down)
            return 0

        lax.fori_loop(0, NXL, body, 0, unroll=2)


def halo_tile(from_c, from_d, parity, k, x):
    low = row_ids() < 4
    c, d = from_c[k, x], from_d[k, x]
    above = jnp.where(parity == 0, c, d)
    below = jnp.where(parity == 0, d, c)
    return (
        jnp.where(low, above, pltpu.roll(below, 4, 0)),
        jnp.where(low, pltpu.roll(above, 4, 0), below),
    )


ORDER = [("e", 0), ("e", 1), ("e", 2), ("h", 0), ("h", 1), ("h", 2), ("p", 0), ("p", 1), ("p", 2), ("c", 2), ("c", 0), ("c", 1)]


def pack_corner(from_c, from_d, out_a, out_b):
    ypar = lax.axis_index("gy") % 2
    parity = lax.axis_index("gx") % 2
    place = {(n, c): (planes, at) for n, c, planes, at in plane_parts()}
    for which, out in enumerate((out_a, out_b)):
        upward = parity == which
        s4 = jnp.where(upward, NXL - 4, 0)
        s3 = jnp.where(upward, NXL - 3, 0)
        for k in range(6):
            pair = [place[ORDER[2 * k]], place[ORDER[2 * k + 1]]]
            for i in range(4):
                tiles = {}
                for j, (planes, at) in enumerate(pair):
                    if i >= planes:
                        continue
                    if planes not in tiles:
                        s = s4 if planes == 4 else s3
                        tiles[planes] = halo_tile(from_c, from_d, ypar, k, s + i)
                    out[at + i] = tiles[planes][j]


def steps_kernel(
    e, h, p, mat, via, fill, perm, cond, stre, rlx, conf,
    got_a, got_b, row_c, row_d, cor_a, cor_b,
    e_out, h_out, p_out,
    ex, hx, px, cells, fills, w, sems,
):
    gx, gy = lax.axis_index("gx"), lax.axis_index("gy")
    nx, ny = lax.axis_size("gx"), lax.axis_size("gy")
    own = pl.ds(HALO, NXL)
    rows = pl.ds(0, NYL)
    loads = []
    for src, dst in ((e, ex), (h, hx), (p, px)):
        loads.append((src, dst.at[:, own, rows]))
    loads += [(mat, cells.at[0, own, rows]), (via, cells.at[1, own, rows]), (fill, fills.at[own, rows])]
    loads = [pltpu.make_async_copy(a, b, sems.at[i]) for i, (a, b) in enumerate(loads)]
    for copy in loads:
        copy.start()

    ext = {"e": ex, "h": hx, "p": px}

    def put(name, c, at, n, rws, value):
        if name == "c":
            if c == 2:
                fills[pl.ds(at, n), rws] = value
            else:
                cells[c, pl.ds(at, n), rws] = value.astype(jnp.int32)
        else:
            ext[name][c, pl.ds(at, n), rws] = value

    for which, (slab, corner) in enumerate(((got_a, cor_a), (got_b, cor_b))):
        from_above = gx % 2 == which
        d4 = jnp.where(from_above, HALO + NXL, 0)
        d3 = jnp.where(from_above, HALO + NXL, 1)
        for name, c, n, at in plane_parts():
            d = d4 if n == 4 else d3
            put(name, c, d, n, slice(0, NYL), slab[at:at + n])
            put(name, c, d, n, slice(NYL, NYE), corner[at:at + n])

    def rows_body(x, _):
        for k in range(6):
            pair = halo_tile(row_c, row_d, gy % 2, k, x)
            for j in range(2):
                name, c = ORDER[2 * k + j]
                if name == "c":
                    if c == 2:
                        fills[x + HALO, NYL:] = pair[j]
                    else:
                        cells[c, x + HALO, NYL:] = pair[j].astype(jnp.int32)
                else:
                    ext[name][c, x + HALO, NYL:] = pair[j]
        return 0

    lax.fori_loop(0, NXL, rows_body, 0, unroll=2)

    for copy in loads:
        copy.wait()

    row = lax.broadcasted_iota(jnp.int32, (NYE, NZ), 0)
    off_above = (row >= NYL) & (row < NYL + 4) & (gy == ny - 1)
    off_below = (row >= NYL + 4) & (gy == 0)
    row_in = jnp.where(off_above | off_below, 0.0, 1.0).astype(F32)
    lane = lax.broadcasted_iota(jnp.int32, (NYE, NZ), 1)
    last, first = lane == NZ - 1, lane == 0

    def plane_in(x):
        out = ((x < HALO) & (gx == 0)) | ((x >= HALO + NXL) & (gx == nx - 1))
        return jnp.where(out, 0.0, 1.0).astype(F32)

    def full(value):
        return jnp.full((8, NZ), value, F32)

    mats = []
    for m in range(3):
        tau = full(rlx[m])
        inv = 1.0 / (2.0 * tau + DT)
        mats.append((full(perm[m]), full(cond[m]) * (DT / 2), (2.0 * tau - DT) * inv, 2.0 * DT * full(stre[m]) * inv, 2.0 * DT * inv))
    lane8 = lax.broadcasted_iota(jnp.int32, (8, NZ), 1)
    tables = []
    for c in range(3):
        table = jnp.zeros((8, NZ), F32)
        for v in range(8):
            table = jnp.where(lane8 == v, conf[v, c], table)
        tables.append(table)

    def coef_body(x, _):
        inside = plane_in(x)
        for t in range(NYE // 8):
            r = slice(8 * t, 8 * t + 8)
            m, v, f = cells[0, x, r], cells[1, x, r], fills[x, r]
            m0, m1 = m == 0, m == 1
            pe, s, kp, bp, omk = (jnp.where(m0, mats[0][i], jnp.where(m1, mats[1][i], mats[2][i])) for i in range(5))
            eps = pe * (1.0 + f)
            inv = 1.0 / (eps + s)
            w[0, x, r] = (eps - s) * inv - inv * bp
            w[1, x, r] = inv * omk
            w[2, x, r] = kp
            w[3, x, r] = bp
            scale = inv * (DT * inside)
            if t == NYE // 8 - 1:
                scale = scale * row_in[r]
            for c in range(3):
                w[4 + c, x, r] = scale * jnp.take_along_axis(tables[c], v, axis=1)
        return 0

    lax.fori_loop(1, NXE - 1, coef_body, 0)

    def yf(a):
        return pltpu.roll(a, NYE - 1, 0)

    def yb(a):
        return pltpu.roll(a, 1, 0)

    def zf(a):
        return jnp.where(last, 0.0, pltpu.roll(a, NZ - 1, 1))

    def zb(a):
        return jnp.where(first, 0.0, pltpu.roll(a, 1, 1))

    def h_plane(x):
        m = row_in * (DT * plane_in(x))
        e0, e1, e2 = ex[0, x], ex[1, x], ex[2, x]
        h0 = hx[0, x] - m * ((yf(e2) - e2) - (zf(e1) - e1))
        h1 = hx[1, x] - m * ((zf(e0) - e0) - (ex[2, x + 1] - e2))
        h2 = hx[2, x] - m * ((ex[1, x + 1] - e1) - (yf(e0) - e0))
        hx[0, x], hx[1, x], hx[2, x] = h0, h1, h2
        return h0, h1, h2

    def e_plane(x, now, before):
        h0, h1, h2 = now
        curl = (
            (h2 - yb(h2)) - (h1 - zb(h1)),
            (h0 - zb(h0)) - (h2 - before[1]),
            (h1 - before[0]) - (h0 - yb(h0)),
        )
        for c in range(3):
            a, b = ex[c, x], px[c, x]
            ex[c, x] = w[0, x] * a + w[1, x] * b + w[4 + c, x] * curl[c]
            px[c, x] = w[2, x] * b + w[3, x] * a

    for step in range(STEPS):
        lo = step
        hi = NXE - 1 - step
        _, h1, h2 = h_plane(lo)

        def body(x, before):
            now = h_plane(x)
            e_plane(x, now, before)
            return now[1], now[2]

        lax.fori_loop(lo + 1, hi, body, (h1, h2))

    stores = []
    for src, dst in ((ex, e_out), (hx, h_out), (px, p_out)):
        stores.append(pltpu.make_async_copy(src.at[:, own, rows], dst, sems.at[len(stores)]))
    for copy in stores:
        copy.start()
    for copy in stores:
        copy.wait()


def shards(efield, hfield, polar, material_map, via_index, fill_fraction, permittivity, conductivity, debye_strength, relax_time, conformal):
    anywhere = pl.BlockSpec(memory_space=pl.ANY)
    vmem = pl.BlockSpec(memory_space=pltpu.VMEM)
    smem = pl.BlockSpec(memory_space=pltpu.SMEM)
    cells = (efield, hfield, polar, material_map, via_index, fill_fraction)
    slab = jax.ShapeDtypeStruct((NMSG, NYL, NZ), F32)
    strip = jax.ShapeDtypeStruct((6, NXL, 8, NZ), F32)
    corner = jax.ShapeDtypeStruct((NMSG, 8, NZ), F32)
    field = jax.ShapeDtypeStruct((3, NXL, NYL, NZ), F32)
    slab_a, slab_b = pl.pallas_call(
        pack_gx, out_shape=(slab, slab), in_specs=[anywhere] * 6, out_specs=(vmem, vmem),
        scratch_shapes=[pltpu.VMEM((2, 2, 3, NYL, NZ), jnp.int32), pltpu.SemaphoreType.DMA((24,))],
        name="pack_gx",
    )(*cells)
    strip_c, strip_d = pl.pallas_call(
        pack_gy, out_shape=(strip, strip), in_specs=[anywhere] * 6, out_specs=(vmem, vmem),
        scratch_shapes=[pltpu.VMEM((2, 10, NXL, 8, NZ), F32), pltpu.VMEM((2, 2, NXL, 8, NZ), jnp.int32), pltpu.SemaphoreType.DMA((12,))],
        name="pack_gy",
    )(*cells)
    got_b = swapped(slab_b, "gx", 1)
    got_a = swapped(slab_a, "gx", 0)
    row_c = swapped(strip_c, "gy", 0)
    row_d = swapped(strip_d, "gy", 1)
    corner_a, corner_b = pl.pallas_call(
        pack_corner, out_shape=(corner, corner), in_specs=[vmem] * 2, out_specs=(vmem, vmem), name="pack_corner",
    )(row_c, row_d)
    cor_b = swapped(corner_b, "gx", 1)
    cor_a = swapped(corner_a, "gx", 0)
    ext = (NXE, NYE, NZ)
    return pl.pallas_call(
        steps_kernel, out_shape=(field,) * 3,
        in_specs=[anywhere] * 6 + [smem] * 5 + [vmem] * 6, out_specs=(anywhere,) * 3,
        scratch_shapes=[
            pltpu.VMEM((3,) + ext, F32), pltpu.VMEM((3,) + ext, F32), pltpu.VMEM((3,) + ext, F32),
            pltpu.VMEM((2,) + ext, jnp.int32), pltpu.VMEM(ext, F32), pltpu.VMEM((7,) + ext, F32),
            pltpu.SemaphoreType.DMA((6,)),
        ],
        compiler_params=pltpu.CompilerParams(vmem_limit_bytes=40 << 20),
        name="steps",
    )(*cells, permittivity, conductivity, debye_strength, relax_time, conformal, got_a, got_b, row_c, row_d, cor_a, cor_b)


def solution(mesh):
    whole, cell = P(None, "gx", "gy", None), P("gx", "gy", None)
    return jax.shard_map(
        shards, mesh=mesh, in_specs=(whole,) * 3 + (cell,) * 3 + (P(),) * 5, out_specs=(whole,) * 3, check_vma=False,
    )
```

time: 142 us -> 56.2 us (0.40)
  other arithmetic: 56.8 us -> 0 us
  Pallas kernels: 0 us -> 25.6 us
  waiting for transfers between devices: 36.5 us -> 14.4 us
  local copies, waits for them, and re-layouts: 17.7 us -> 1.14 us
  starting transfers between devices: 28.5 us -> 13.8 us
    unnamed x6 -> x0, other arithmetic: 32.7 us -> none
    pallas_call x0 -> x4, Pallas kernels: none -> 25.6 us  [the longest x1 18.3 us: shards(): pl.pallas_call(steps_kernel, out_shape=(field,) * 3, in_specs=[anywhere]...]
    ppermute x10 -> x6, waiting for transfers between devices: 36.5 us -> 14.4 us  [swapped(): return lax.ppermute(value, axis, pairs)]
    ppermute x10 -> x6, starting transfers between devices: 28.5 us -> 13.8 us  [swapped(): return lax.ppermute(value, axis, pairs)]
    slice x53 -> x0, local copies, waits for them, and re-layouts: 12.2 us -> none  [the longest x6 7.71 us: select(): table[entry]]
    concatenate x2 -> x0, other arithmetic: 10.2 us -> none  [the longest x1 9.29 us: cell_stack(): return jnp.concatenate([efield, hfield, polar, coef], 0)]
    sub x10 -> x0, other arithmetic: 5.29 us -> none  [the longest x3 3.44 us: shards(): coef[0] * elec + coef[4:7] * curl_h(magn, y_prev, x_zero)]
    unnamed x27, local copies, waits for them, and re-layouts: 4.93 us -> 1.14 us
  transfers between devices with their start and end apart: 10 -> 6, of which waited for: 10 -> 3; matrix products, arithmetic and copies ran while one was open for 2% -> 0% of each run, Pallas kernels for 0% -> 8%
where the time goes in v1:
time: 56.2 us; the launch traced here: 55.8 us
  Pallas kernels  25.6 us (46%)
  waiting for transfers between devices  14.4 us (26%)
  starting transfers between devices  13.8 us (25%)
  local copies, waits for them, and re-layouts  1.14 us (2%)
  between operations  0.86 us (2%)
    pallas_call x1, Pallas kernels, shards(): pl.pallas_call(steps_kernel, out_shape=(field,) * 3, in_specs=[anywhere]...  18.3 us
    ppermute x6, waiting for transfers between devices, swapped(): return lax.ppermute(value, axis, pairs)  14.4 us
    ppermute x6, starting transfers between devices, swapped(): return lax.ppermute(value, axis, pairs)  13.8 us
    pallas_call x1, Pallas kernels, shards(): pl.pallas_call(pack_gy, out_shape=(strip, strip), in_specs=[anywhere] * 6...  2.78 us
    pallas_call x1, Pallas kernels, shards(): pl.pallas_call(pack_gx, out_shape=(slab, slab), in_specs=[anywhere] * 6,...  2.58 us
    pallas_call x1, Pallas kernels, shards(): pl.pallas_call(pack_corner, out_shape=(corner, corner), in_specs=[vmem] *...  1.88 us
    unnamed x27, local copies, waits for them, and re-layouts  1.14 us
  transfers between devices with their start and end apart: 6, of which 3 were waited for; matrix products, arithmetic and copies ran while one was open for 0% of the time, Pallas kernels for 8%

profile of v1, /device:TPU:122, one launch (start us, length us, event | category | flops | bytes accessed | tf_op | source)
XLA Modules:
  0.0 55.8 jit_solution(5666902803205807190)
XLA Ops:
  0.6 2.6 %pack_gx.1 = (f32[41,32,128]{2,1,0:T(8,128)}, f32[41,32,128]{2,1,0:T(8,128)}) custom-call(f32[3,16,32,128]{3,2,1,0:T(8,128)} %e.5, f32[3,16,32,128]{3,2,1,0:T(8,128)} %h.5, f32[3,16,32,128]{3,2,1,0:T(8,128)} %p.5, s32[16,32,128]{2,1,0:T(8,128)} %mat.5, s32[16,32,128]{2,1,0:T(8,128)} %via.5, f32[16,32,128]{2,1,0:T(8,128)} %fill.5), custom_call_target="tpu_custom_call" | custom-call | tf_op jit(solution)/shard_map/pack_gx/pallas_call | solution.py:302
  3.2 0.8 %collective-permute-start = (f32[41,32,128]{2,1,0:T(8,128)}, f32[41,32,128]{2,1,0:T(8,128)}, u32[]{:S(2)}, u32[]{:S(2)}) collective-permute-start(f32[41,32,128]{2,1,0:T(8,128)} %get-tuple-element.9), channel_id=1, source_target_pairs={{0,8},{8,0},{16,24},{24,16},{32,40},{40,32},{48,56},{56,48},{64,72... | collective-permute-start | bytes 2015240 | tf_op jit(solution)/shard_map/ppermute | solution.py:24
  4.0 5.5 %collective-permute-start.1 = (f32[41,32,128]{2,1,0:T(8,128)}, f32[41,32,128]{2,1,0:T(8,128)}, u32[]{:S(2)}, u32[]{:S(2)}) collective-permute-start(f32[41,32,128]{2,1,0:T(8,128)} %get-tuple-element.10), channel_id=1, source_target_pairs={{8,16},{16,8},{24,32},{32,24},{40,48},{48,40},{56,64},{64,56},{72,... | collective-permute-start | bytes 2015240 | tf_op jit(solution)/shard_map/ppermute | solution.py:24
  9.6 0.0 copy-start.1
  9.6 0.0 copy-start.2
  9.6 0.0 copy-start.3
  9.6 0.0 copy-start.4
  9.6 0.0 copy-start.5
  9.6 2.8 %pack_gy.1 = (f32[6,16,8,128]{3,2,1,0:T(8,128)}, f32[6,16,8,128]{3,2,1,0:T(8,128)}) custom-call(f32[3,16,32,128]{3,2,1,0:T(8,128)} %e.5, f32[3,16,32,128]{3,2,1,0:T(8,128)} %h.5, f32[3,16,32,128]{3,2,1,0:T(8,128)} %p.5, s32[16,32,128]{2,1,0:T(8,128)} %mat.5, s32[16,32,128]{2,1,0:T(8,128)} %via.5, f32[16,32,128]{2,1,0:T(8,128)} %fill.5), custom_call_target="tpu_custom_call" | custom-call | tf_op jit(solution)/shard_map/pack_gy/pallas_call | solution.py:307
  12.4 0.0 copy-start
  12.4 0.1 collective-permute-start.2
  12.5 2.5 %collective-permute-start.3 = (f32[6,16,8,128]{3,2,1,0:T(8,128)}, f32[6,16,8,128]{3,2,1,0:T(8,128)}, u32[]{:S(2)}, u32[]{:S(2)}) collective-permute-start(f32[6,16,8,128]{3,2,1,0:T(8,128)} %get-tuple-element.12), channel_id=1, source_target_pairs={{1,2},{2,1},{3,4},{4,3},{5,6},{6,5},{9,10},{10,9},{11,12},{12,11},... | collective-permute-start | bytes 1179656 | tf_op jit(solution)/shard_map/ppermute | solution.py:24
  15.1 0.0 collective-permute-done.2.from_c.row_c
  15.1 0.0 copy-start.6
  15.1 7.0 %collective-permute-done.3.from_d.row_d = f32[6,16,8,128]{3,2,1,0:T(8,128)} collective-permute-done((f32[6,16,8,128]{3,2,1,0:T(8,128)}, f32[6,16,8,128]{3,2,1,0:T(8,128)}, u32[]{:S(2)}, u32[]{:S(2)}) %collective-permute-start.3) | collective-permute-done | bytes 393248 | tf_op jit(solution)/shard_map/ppermute | solution.py:24
  22.1 0.0 copy-done.6
  22.1 1.9 %pack_corner.1 = (f32[41,8,128]{2,1,0:T(8,128)}, f32[41,8,128]{2,1,0:T(8,128)}) custom-call(f32[6,16,8,128]{3,2,1,0:T(8,128)} %copy-done.6, f32[6,16,8,128]{3,2,1,0:T(8,128)} %collective-permute-done.3.from_d.row_d), custom_call_target="tpu_custom_call" | custom-call | tf_op jit(solution)/shard_map/pack_corner/pallas_call | solution.py:316
  24.0 0.0 copy-start.12
  24.0 0.0 collective-permute-start.4
  24.0 0.0 copy-start.8
  24.0 0.0 copy-start.9
  24.0 0.0 copy-start.10
  24.0 0.0 copy-start.11
  24.0 4.9 %collective-permute-start.5 = (f32[41,8,128]{2,1,0:T(8,128)}, f32[41,8,128]{2,1,0:T(8,128)S(1)}, u32[]{:S(2)}, u32[]{:S(2)}) collective-permute-start(f32[41,8,128]{2,1,0:T(8,128)} %get-tuple-element.14), channel_id=1, source_target_pairs={{8,16},{16,8},{24,32},{32,24},{40,48},{48,40},{56,64},{64,56},{72,... | collective-permute-start | bytes 503816 | tf_op jit(solution)/shard_map/ppermute | solution.py:24
  28.9 0.0 copy-done.12
  28.9 0.1 copy.14.conf
  29.0 2.0 %collective-permute-done.4.cor_a = f32[41,8,128]{2,1,0:T(8,128)S(1)} collective-permute-done((f32[41,8,128]{2,1,0:T(8,128)}, f32[41,8,128]{2,1,0:T(8,128)S(1)}, u32[]{:S(2)}, u32[]{:S(2)}) %collective-permute-start.4) | collective-permute-done | bytes 167968 | tf_op jit(solution)/shard_map/ppermute | solution.py:24
  31.0 5.4 %collective-permute-done.5.cor_b = f32[41,8,128]{2,1,0:T(8,128)S(1)} collective-permute-done((f32[41,8,128]{2,1,0:T(8,128)}, f32[41,8,128]{2,1,0:T(8,128)S(1)}, u32[]{:S(2)}, u32[]{:S(2)}) %collective-permute-start.5) | collective-permute-done | bytes 167968 | tf_op jit(solution)/shard_map/ppermute | solution.py:24
  36.4 0.0 collective-permute-done.got_a
  36.4 0.0 collective-permute-done.1.got_b
  36.4 0.0 copy-done.1
  36.4 0.0 copy-done.2
  36.4 0.0 copy-done.3
  36.4 0.0 copy-done.4
  36.5 0.0 copy-done.5
  36.5 0.0 copy-done
  36.5 0.0 copy-done.8
  36.5 0.0 copy-done.9
  36.5 0.0 copy-done.10
  36.5 0.0 copy-done.11
  36.5 0.0 copy-start.7
  36.5 1.0 %copy-done.7 = f32[6,16,8,128]{3,2,1,0:T(8,128)S(1)} copy-done((f32[6,16,8,128]{3,2,1,0:T(8,128)S(1)}, f32[6,16,8,128]{3,2,1,0:T(8,128)}, u32[]{:S(2)}) %copy-start.7) | copy-done | bytes 393240
  37.5 18.3 %steps.1 = (f32[3,16,32,128]{3,2,1,0:T(8,128)}, f32[3,16,32,128]{3,2,1,0:T(8,128)}, f32[3,16,32,128]{3,2,1,0:T(8,128)}) custom-call(f32[3,16,32,128]{3,2,1,0:T(8,128)S(1)} %copy-done, f32[3,16,32,128]{3,2,1,0:T(8,128)S(1)} %copy-done.1, f32[3,16,32,128]{3,2,1,0:T(8,128)S(1)} %copy-done.2, s32[16,32,128]{2,1,0:T(8,128)S(1)} %copy-done.3, ...), custom_call_target="tpu_custom_call" | custom-call | tf_op jit(solution)/shard_map/steps/pallas_call | solution.py:322
Async XLA Ops:
  3.2 33.2 %collective-permute-start = (f32[41,32,128]{2,1,0:T(8,128)}, f32[41,32,128]{2,1,0:T(8,128)}, u32[]{:S(2)}, u32[]{:S(2)}) collective-permute-start(f32[41,32,128]{2,1,0:T(8,128)} %get-tuple-element.9), channel_id=1, source_target_pairs={{0,8},{8,0},{16,24},{24,16},{32,40},{40,32},{48,56},{56,48},{64,72... | collective-permute-start | bytes 2015240 | tf_op jit(solution)/shard_map/ppermute | solution.py:24
  4.0 32.4 %collective-permute-start.1 = (f32[41,32,128]{2,1,0:T(8,128)}, f32[41,32,128]{2,1,0:T(8,128)}, u32[]{:S(2)}, u32[]{:S(2)}) collective-permute-start(f32[41,32,128]{2,1,0:T(8,128)} %get-tuple-element.10), channel_id=1, source_target_pairs={{8,16},{16,8},{24,32},{32,24},{40,48},{48,40},{56,64},{64,56},{72,... | collective-permute-start | bytes 2015240 | tf_op jit(solution)/shard_map/ppermute | solution.py:24
  9.6 26.8 %copy-start.1 = (f32[3,16,32,128]{3,2,1,0:T(8,128)S(1)}, f32[3,16,32,128]{3,2,1,0:T(8,128)}, u32[]{:S(2)}) copy-start(f32[3,16,32,128]{3,2,1,0:T(8,128)} %h.5) | copy-start | bytes 2359300
  9.6 26.8 %copy-start.2 = (f32[3,16,32,128]{3,2,1,0:T(8,128)S(1)}, f32[3,16,32,128]{3,2,1,0:T(8,128)}, u32[]{:S(2)}) copy-start(f32[3,16,32,128]{3,2,1,0:T(8,128)} %p.5) | copy-start | bytes 2359300
  9.6 26.8 %copy-start.3 = (s32[16,32,128]{2,1,0:T(8,128)S(1)}, s32[16,32,128]{2,1,0:T(8,128)}, u32[]{:S(2)}) copy-start(s32[16,32,128]{2,1,0:T(8,128)} %mat.5) | copy-start | bytes 786436
  9.6 26.8 %copy-start.4 = (s32[16,32,128]{2,1,0:T(8,128)S(1)}, s32[16,32,128]{2,1,0:T(8,128)}, u32[]{:S(2)}) copy-start(s32[16,32,128]{2,1,0:T(8,128)} %via.5) | copy-start | bytes 786436
  9.6 26.8 %copy-start.5 = (f32[16,32,128]{2,1,0:T(8,128)S(1)}, f32[16,32,128]{2,1,0:T(8,128)}, u32[]{:S(2)}) copy-start(f32[16,32,128]{2,1,0:T(8,128)} %fill.5) | copy-start | bytes 786436
  12.4 24.0 %copy-start = (f32[3,16,32,128]{3,2,1,0:T(8,128)S(1)}, f32[3,16,32,128]{3,2,1,0:T(8,128)}, u32[]{:S(2)}) copy-start(f32[3,16,32,128]{3,2,1,0:T(8,128)} %e.5) | copy-start | bytes 2359300
  12.4 2.6 %collective-permute-start.2 = (f32[6,16,8,128]{3,2,1,0:T(8,128)}, f32[6,16,8,128]{3,2,1,0:T(8,128)S(1)}, u32[]{:S(2)}, u32[]{:S(2)}) collective-permute-start(f32[6,16,8,128]{3,2,1,0:T(8,128)} %get-tuple-element.11), channel_id=1, source_target_pairs={{0,1},{1,0},{2,3},{3,2},{4,5},{5,4},{6,7},{7,6},{8,9},{9,8},{10,11... | collective-permute-start | bytes 1179656 | tf_op jit(solution)/shard_map/ppermute | solution.py:24
  12.5 9.5 %collective-permute-start.3 = (f32[6,16,8,128]{3,2,1,0:T(8,128)}, f32[6,16,8,128]{3,2,1,0:T(8,128)}, u32[]{:S(2)}, u32[]{:S(2)}) collective-permute-start(f32[6,16,8,128]{3,2,1,0:T(8,128)} %get-tuple-element.12), channel_id=1, source_target_pairs={{1,2},{2,1},{3,4},{4,3},{5,6},{6,5},{9,10},{10,9},{11,12},{12,11},... | collective-permute-start | bytes 1179656 | tf_op jit(solution)/shard_map/ppermute | solution.py:24
  15.1 7.0 %copy-start.6 = (f32[6,16,8,128]{3,2,1,0:T(8,128)}, f32[6,16,8,128]{3,2,1,0:T(8,128)S(1)}, u32[]{:S(2)}) copy-start(f32[6,16,8,128]{3,2,1,0:T(8,128)S(1)} %collective-permute-done.2.from_c.row_c) | copy-start | bytes 1179652
  24.0 4.9 %copy-start.12 = (f32[8,3]{0,1:T(4,128)S(1)}, f32[8,3]{0,1:T(4,128)}, u32[]{:S(2)}) copy-start(f32[8,3]{0,1:T(4,128)} %param.21) | copy-start | bytes 292
  24.0 7.1 %collective-permute-start.4 = (f32[41,8,128]{2,1,0:T(8,128)}, f32[41,8,128]{2,1,0:T(8,128)S(1)}, u32[]{:S(2)}, u32[]{:S(2)}) collective-permute-start(f32[41,8,128]{2,1,0:T(8,128)} %get-tuple-element.13), channel_id=1, source_target_pairs={{0,8},{8,0},{16,24},{24,16},{32,40},{40,32},{48,56},{56,48},{64,72... | collective-permute-start | bytes 503816 | tf_op jit(solution)/shard_map/ppermute | solution.py:24
  24.0 12.5 %copy-start.8 = (f32[3]{0:T(128)S(1)}, f32[3]{0:T(128)}, u32[]{:S(2)}) copy-start(f32[3]{0:T(128)} %perm.1) | copy-start | bytes 40
  24.0 12.5 %copy-start.9 = (f32[3]{0:T(128)S(1)}, f32[3]{0:T(128)}, u32[]{:S(2)}) copy-start(f32[3]{0:T(128)} %cond.1) | copy-start | bytes 40
  24.0 12.5 %copy-start.10 = (f32[3]{0:T(128)S(1)}, f32[3]{0:T(128)}, u32[]{:S(2)}) copy-start(f32[3]{0:T(128)} %stre.1) | copy-start | bytes 40
  24.0 12.5 %copy-start.11 = (f32[3]{0:T(128)S(1)}, f32[3]{0:T(128)}, u32[]{:S(2)}) copy-start(f32[3]{0:T(128)} %rlx.1) | copy-start | bytes 40
  24.0 12.4 %collective-permute-start.5 = (f32[41,8,128]{2,1,0:T(8,128)}, f32[41,8,128]{2,1,0:T(8,128)S(1)}, u32[]{:S(2)}, u32[]{:S(2)}) collective-permute-start(f32[41,8,128]{2,1,0:T(8,128)} %get-tuple-element.14), channel_id=1, source_target_pairs={{8,16},{16,8},{24,32},{32,24},{40,48},{48,40},{56,64},{64,56},{72,... | collective-permute-start | bytes 503816 | tf_op jit(solution)/shard_map/ppermute | solution.py:24
  36.5 1.0 %copy-start.7 = (f32[6,16,8,128]{3,2,1,0:T(8,128)S(1)}, f32[6,16,8,128]{3,2,1,0:T(8,128)}, u32[]{:S(2)}) copy-start(f32[6,16,8,128]{3,2,1,0:T(8,128)} %copy-done.6) | copy-start | bytes 1179652

commit v2 on v0

v2 whole, which is shorter than its diff:
```python
import jax
import jax.numpy as jnp
from jax import lax
from jax.experimental import pallas as pl
from jax.experimental.pallas import tpu as pltpu
from jax.sharding import PartitionSpec as P

DT = 0.55
F32 = jnp.float32

NX, NY, NZ = 16, 32, 128
LOW, HIGH = 3, 2
R0, RH, RE = 8, 8 + NY, 16 + NY
EXT = (NX + LOW + HIGH, RE + 8, NZ)
TILES = (RE - R0) // 8
MSG1, MSG2 = 18, 8
MSG2_ROWS = MSG2 * (RE - R0) + MSG1 * 8

ORDER = (("e", 0), ("e", 1), ("e", 2), ("h", 0), ("h", 1), ("h", 2), ("p", 0), ("p", 1), ("p", 2), ("f", 0), ("c", 0), ("c", 1))


def swapped(value, axis, first):
    pairs = []
    for low in range(first, lax.axis_size(axis) - 1, 2):
        pairs += [(low, low + 1), (low + 1, low)]
    return lax.ppermute(value, axis, pairs)


def tile_iota(dim):
    return lax.broadcasted_iota(jnp.int32, (8, NZ), dim)


def materials(perm, cond, stre, rlx):
    out = []
    for m in range(3):
        tau = jnp.full((8, NZ), rlx[m], F32)
        inv = 1.0 / (2.0 * tau + DT)
        out.append((
            jnp.full((8, NZ), perm[m], F32), jnp.full((8, NZ), cond[m] * (DT / 2), F32),
            (2.0 * tau - DT) * inv, jnp.full((8, NZ), stre[m], F32) * (2.0 * DT) * inv, 2.0 * DT * inv,
        ))
    return out


def pick(mats, m, i):
    return jnp.where(m == 0, mats[0][i], jnp.where(m == 1, mats[1][i], mats[2][i]))


def via_tables(conf):
    lane = tile_iota(1)
    tables = []
    for c in range(3):
        table = jnp.zeros((8, NZ), F32)
        for v in range(8):
            table = jnp.where(lane == v, conf[c, v], table)
        tables.append(table)
    return tables


class Block:
    def __init__(self, ex, hx, px, cx, fx, w=None):
        self.e, self.h, self.p, self.c, self.f, self.w = ex, hx, px, cx, fx, w

    def masks(self):
        gy = lax.axis_index("gy")
        row = tile_iota(0)
        out = ((row < 4) & (gy == lax.axis_size("gy") - 1)) | ((row >= 4) & (gy == 0))
        self.row_in = jnp.where(out, 0.0, 1.0).astype(F32)
        lane = tile_iota(1)
        self.last, self.first = lane == NZ - 1, lane == 0

    def plane_in(self, x):
        if not isinstance(x, int) or 0 <= x < NX:
            return None
        gx = lax.axis_index("gx")
        out = gx == 0 if x < 0 else gx == lax.axis_size("gx") - 1
        return jnp.where(out, 0.0, 1.0).astype(F32)

    def zf(self, a):
        return jnp.where(self.last, 0.0, pltpu.roll(a, NZ - 1, 1))

    def zb(self, a):
        return jnp.where(self.first, 0.0, pltpu.roll(a, 1, 1))

    def coef(self, x, mats, tables):
        i = x + LOW
        inside = self.plane_in(x)
        for t in range(TILES):
            r = slice(R0 + 8 * t, R0 + 8 * t + 8)
            m, v, f = self.c[0, i, r], self.c[1, i, r], self.f[0, i, r]
            pe, s, kp, bp, omk = (pick(mats, m, k) for k in range(5))
            eps = pe * (1.0 + f)
            inv = 1.0 / (eps + s)
            self.w[0, i, r] = (eps - s) * inv - inv * bp
            self.w[1, i, r] = inv * omk
            self.w[2, i, r] = kp
            self.w[3, i, r] = bp
            scale = inv * DT if inside is None else inv * (DT * inside)
            if t == TILES - 1:
                scale = scale * self.row_in
            for c in range(3):
                self.w[4 + c, i, r] = scale * jnp.take_along_axis(tables[c], v, axis=1)

    def guard_e(self, i):
        for c in (0, 2):
            self.e[c, i, RE:RE + 1] = self.e[c, i, R0:R0 + 1]

    def h_plane(self, x):
        i = x + LOW
        e, h = self.e, self.h
        inside = self.plane_in(x)
        for t in range(TILES):
            a = R0 + 8 * t
            r, up = slice(a, a + 8), slice(a + 1, a + 9)
            e0, e1, e2 = e[0, i, r], e[1, i, r], e[2, i, r]
            m = DT if inside is None else DT * inside
            if t == TILES - 1:
                m = self.row_in * m
            h0 = h[0, i, r] - m * ((e[2, i, up] - e2) - (self.zf(e1) - e1))
            h1 = h[1, i, r] - m * ((self.zf(e0) - e0) - (e[2, i + 1, r] - e2))
            h2 = h[2, i, r] - m * ((e[1, i + 1, r] - e1) - (e[0, i, up] - e0))
            h[0, i, r], h[1, i, r], h[2, i, r] = h0, h1, h2
        h[0, i, R0 - 1:R0] = h0[7:8]
        h[2, i, R0 - 1:R0] = h2[7:8]

    def e_plane(self, x):
        i = x + LOW
        e, h, p, w = self.e, self.h, self.p, self.w
        for t in range(TILES):
            a = R0 + 8 * t
            r, down = slice(a, a + 8), slice(a - 1, a + 7)
            h0, h1, h2 = h[0, i, r], h[1, i, r], h[2, i, r]
            curl = (
                (h2 - h[2, i, down]) - (h1 - self.zb(h1)),
                (h0 - self.zb(h0)) - (h2 - h[2, i - 1, r]),
                (h1 - h[1, i - 1, r]) - (h0 - h[0, i, down]),
            )
            w0, w1, w2, w3 = (w[k, i, r] for k in range(4))
            for c in range(3):
                ec, pc = e[c, i, r], p[c, i, r]
                new = w0 * ec + w1 * pc + w[4 + c, i, r] * curl[c]
                e[c, i, r] = new
                p[c, i, r] = w2 * pc + w3 * ec
                if t == 0 and c != 1:
                    e[c, i, RE:RE + 1] = new[0:1]

    def sweep(self, h_planes, e_planes):
        for x in range(min(h_planes[0], e_planes[0]), max(h_planes[1], e_planes[1]) + 1):
            if h_planes[0] <= x <= h_planes[1]:
                self.h_plane(x)
            if e_planes[0] <= x <= e_planes[1]:
                self.e_plane(x)

    def long_sweep(self, h_planes, e_planes):
        lo, hi = max(h_planes[0], e_planes[0]), min(h_planes[1], e_planes[1])
        for x in range(h_planes[0], lo):
            self.h_plane(x)

        def body(x, _):
            self.h_plane(x)
            self.e_plane(x)
            return 0

        lax.fori_loop(lo, hi + 1, body, 0)
        for x in range(hi + 1, e_planes[1] + 1):
            self.e_plane(x)


def copy_all(pairs, sems):
    copies = [pltpu.make_async_copy(a, b, sems.at[k]) for k, (a, b) in enumerate(pairs)]
    for copy in copies:
        copy.start()
    return copies


def load_and_pack(e, h, p, mat, via, fill, perm, cond, stre, rlx, ex, hx, px, cx, fx, out_c, out_d, out_a, out_b, sems):
    own, rows = pl.ds(LOW, NX), pl.ds(R0, NY)
    pairs = [(e, ex.at[:, own, rows]), (h, hx.at[:, own, rows]), (p, px.at[:, own, rows])]
    pairs += [(mat, cx.at[0, own, rows]), (via, cx.at[1, own, rows]), (fill, fx.at[0, own, rows])]
    copies = copy_all(pairs, sems)
    mats = materials(perm, cond, stre, rlx)
    for copy in copies:
        copy.wait()
    refs = {"e": ex, "h": hx, "p": px, "c": cx, "f": fx}
    low = tile_iota(0) < 4
    gy_odd, gx_odd = lax.axis_index("gy") % 2, lax.axis_index("gx") % 2

    def strip(x, r, out, upward):
        tiles = [refs[n][c, x + LOW, r:r + 8].astype(F32) for n, c in ORDER]
        for k in range(6):
            a, b = tiles[2 * k], tiles[2 * k + 1]
            if upward:
                out[k, x] = jnp.where(low, pltpu.roll(a, 4, 0), b)
            else:
                out[k, x] = jnp.where(low, a, pltpu.roll(b, 4, 0))

    def strips(up, down):
        def body(x, _):
            strip(x, RH - 8, up, True)
            strip(x, R0, down, False)
            return 0

        lax.fori_loop(0, NX, body, 0, unroll=2)

    @pl.when(gy_odd == 0)
    def _():
        strips(out_c, out_d)

    @pl.when(gy_odd == 1)
    def _():
        strips(out_d, out_c)

    own_rows = slice(R0, RH)

    def slab(out, d1, d2):
        for c in range(3):
            out[c] = ex[c, d1, own_rows]
            out[3 + c] = px[c, d1, own_rows]
            out[15 + c] = hx[c, d1, own_rows]
        for k, i in ((6, d1), (9, d2)):
            out[k] = cx[0, i, own_rows].astype(F32)
            out[k + 1] = cx[1, i, own_rows].astype(F32)
            out[k + 2] = fx[0, i, own_rows]
        for t in range(NY // 8):
            r = slice(R0 + 8 * t, R0 + 8 * t + 8)
            m = cx[0, d2, r]
            kp, bp = pick(mats, m, 2), pick(mats, m, 3)
            for c in range(3):
                out[12 + c, 8 * t:8 * t + 8] = kp * px[c, d2, r] + bp * ex[c, d2, r]

    @pl.when(gx_odd == 0)
    def _():
        slab(out_a, LOW + NX - 1, LOW + NX - 2)
        slab(out_b, LOW, LOW + 1)

    @pl.when(gx_odd == 1)
    def _():
        slab(out_b, LOW + NX - 1, LOW + NX - 2)
        slab(out_a, LOW, LOW + 1)


def first_edges(row_c, row_d, perm, cond, stre, rlx, conf, *refs):
    ex, hx, px, cx, fx, w, out_a, out_b = refs[5:]
    b = Block(ex, hx, px, cx, fx, w)
    b.masks()
    named = {"e": ex, "h": hx, "p": px, "c": cx, "f": fx}
    low = tile_iota(0) < 4
    gy_odd, gx_odd = lax.axis_index("gy") % 2, lax.axis_index("gx") % 2

    def rows_body(x, above_ref, below_ref):
        for k in range(6):
            above, below = above_ref[k, x], below_ref[k, x]
            both = (jnp.where(low, above, pltpu.roll(below, 4, 0)), jnp.where(low, pltpu.roll(above, 4, 0), below))
            for (n, c), tile in zip(ORDER[2 * k:2 * k + 2], both):
                named[n][c, x + LOW, RH:RE] = tile.astype(jnp.int32) if n == "c" else tile
        for c in (0, 2):
            ex[c, x + LOW, RE:RE + 1] = ex[c, x + LOW, R0:R0 + 1]
            hx[c, x + LOW, R0 - 1:R0] = hx[c, x + LOW, RE - 1:RE]

    def all_rows(above_ref, below_ref):
        def body(x, _):
            rows_body(x, above_ref, below_ref)
            return 0

        lax.fori_loop(0, NX, body, 0, unroll=2)

    @pl.when(gy_odd == 0)
    def _():
        all_rows(row_c, row_d)

    @pl.when(gy_odd == 1)
    def _():
        all_rows(row_d, row_c)

    mats, tables = materials(perm, cond, stre, rlx), via_tables(conf)
    for x in (1, 2, NX - 3, NX - 2):
        b.coef(x, mats, tables)
    b.h_plane(0)
    for x in (1, 2):
        b.h_plane(x)
        b.e_plane(x)
    b.h_plane(1)
    b.h_plane(NX - 4)
    for x in (NX - 3, NX - 2):
        b.h_plane(x)
        b.e_plane(x)
    b.h_plane(NX - 3)

    n = RE - R0

    def message(out, upward):
        d1, d2, d3 = (LOW + NX - 1, LOW + NX - 2, LOW + NX - 3) if upward else (LOW, LOW + 1, None)
        if upward:
            planes = [(hx, c, d2) for c in range(3)] + [(ex, c, d2) for c in range(3)] + [(hx, c, d3) for c in (1, 2)]
        else:
            planes = [(hx, c, d1) for c in range(3)] + [(hx, c, d2) for c in range(3)] + [(ex, c, d2) for c in (1, 2)]
        for k, (ref, c, i) in enumerate(planes):
            out[n * k:n * k + n] = ref[c, i, R0:RE]
        tiles = [(ex, c, d1) for c in range(3)] + [(px, c, d1) for c in range(3)]
        for i in (d1, d2):
            tiles += [(cx, 0, i), (cx, 1, i), (fx, 0, i)]
        tiles += [(px, c, d2) for c in range(3)] + [(hx, c, d1) for c in range(3)]
        for k, (ref, c, i) in enumerate(tiles):
            at = MSG2 * n + 8 * k
            out[at:at + 8] = ref[c, i, RH:RE].astype(F32)

    @pl.when(gx_odd == 0)
    def _():
        message(out_a, True)
        message(out_b, False)

    @pl.when(gx_odd == 1)
    def _():
        message(out_b, True)
        message(out_a, False)


def interior(cx, fx, perm, cond, stre, rlx, conf, *refs):
    ex, hx, px, w = refs[4:]
    b = Block(ex, hx, px, cx, fx, w)
    b.masks()
    mats, tables = materials(perm, cond, stre, rlx), via_tables(conf)
    b.coef(0, mats, tables)
    b.coef(NX - 1, mats, tables)

    def body(x, _):
        b.coef(x, mats, tables)
        return 0

    lax.fori_loop(3, NX - 3, body, 0)
    b.long_sweep((3, NX - 5), (3, NX - 4))
    b.long_sweep((2, NX - 4), (2, NX - 3))
    b.long_sweep((2, NX - 4), (3, NX - 4))
    b.long_sweep((3, NX - 5), (4, NX - 5))


def last_edges(got1_a, got1_b, got2_a, got2_b, perm, cond, stre, rlx, conf, *refs):
    e_out, h_out, p_out, ex, hx, px, cx, fx, w, sems = refs[6:]
    b = Block(ex, hx, px, cx, fx, w)
    b.masks()
    rows = pl.ds(R0, NY)
    outs = ((ex, e_out), (hx, h_out), (px, p_out))

    def part(first, count):
        return [(src.at[:, pl.ds(LOW + first, count), rows], dst.at[:, pl.ds(first, count)]) for src, dst in outs]

    done = copy_all(part(4, NX - 8), sems.at[pl.ds(0, 3)])
    gx_odd = lax.axis_index("gx") % 2
    n = RE - R0
    own_rows, halo_rows = slice(R0, RH), slice(RH, RE)

    def take(m1, m2, below):
        d1, d2, d3 = (LOW - 1, LOW - 2, LOW - 3) if below else (LOW + NX, LOW + NX + 1, None)

        def put(ref, c, i, k):
            at = MSG2 * n + 8 * k
            head, tail = m1[k], m2[at:at + 8]
            if ref is cx:
                head, tail = head.astype(jnp.int32), tail.astype(jnp.int32)
            ref[c, i, own_rows] = head
            ref[c, i, halo_rows] = tail

        for c in range(3):
            put(ex, c, d1, c)
            put(px, c, d1, 3 + c)
            put(px, c, d2, 12 + c)
            if below:
                put(hx, c, d1, 15 + c)
        for k, i in ((6, d1), (9, d2)):
            put(cx, 0, i, k)
            put(cx, 1, i, k + 1)
            put(fx, 0, i, k + 2)
        if below:
            planes = [(hx, c, d2) for c in range(3)] + [(ex, c, d2) for c in range(3)] + [(hx, c, d3) for c in (1, 2)]
        else:
            planes = [(hx, c, d1) for c in range(3)] + [(hx, c, d2) for c in range(3)] + [(ex, c, d2) for c in (1, 2)]
        for k, (ref, c, i) in enumerate(planes):
            ref[c, i, R0:RE] = m2[n * k:n * k + n]
        for i in (d1, d2):
            for c in (0, 2):
                ex[c, i, RE:RE + 1] = ex[c, i, R0:R0 + 1]
                hx[c, i, R0 - 1:R0] = hx[c, i, RE - 1:RE]

    @pl.when(gx_odd == 0)
    def _():
        take(got1_a, got2_a, False)
        take(got1_b, got2_b, True)

    @pl.when(gx_odd == 1)
    def _():
        take(got1_b, got2_b, False)
        take(got1_a, got2_a, True)

    mats, tables = materials(perm, cond, stre, rlx), via_tables(conf)
    for x in (-2, -1, NX, NX + 1):
        b.coef(x, mats, tables)
    m = NX - 16
    b.sweep((-1, -1), (-1, 0))
    b.sweep((-2, 0), (-2, 1))
    b.sweep((-2, 1), (-1, 2))
    b.sweep((-1, 2), (0, 3))
    for copy in done:
        copy.wait()
    done = copy_all(part(0, 4), sems.at[pl.ds(0, 3)])
    b.sweep((m + 15, m + 15), (m + 15, m + 16))
    b.sweep((m + 14, m + 16), (m + 14, m + 17))
    b.sweep((m + 13, m + 16), (m + 13, m + 16))
    b.sweep((m + 12, m + 15), (m + 12, m + 15))
    done += copy_all(part(NX - 4, 4), sems.at[pl.ds(3, 3)])
    for copy in done:
        copy.wait()


def shards(efield, hfield, polar, material_map, via_index, fill_fraction, permittivity, conductivity, debye_strength, relax_time, conformal):
    vmem = pl.BlockSpec(memory_space=pltpu.VMEM)
    smem = pl.BlockSpec(memory_space=pltpu.SMEM)
    hbm = pl.BlockSpec(memory_space=pltpu.HBM)
    conformal = conformal.T
    cells = (efield, hfield, polar, material_map, via_index, fill_fraction)
    cells = tuple(pltpu.with_memory_space_constraint(a, pltpu.HBM) for a in cells)
    tables = (permittivity, conductivity, debye_strength, relax_time)
    tables = tuple(pltpu.with_memory_space_constraint(a, pltpu.HBM) for a in tables)
    shape = jax.ShapeDtypeStruct
    field, slab1 = shape((3,) + EXT, F32), shape((MSG1, NY, NZ), F32)
    slab2, strip = shape((MSG2_ROWS, NZ), F32), shape((6, NX, 8, NZ), F32)
    ints, fill, coef = shape((2,) + EXT, jnp.int32), shape((1,) + EXT, F32), shape((7,) + EXT, F32)
    result = shape((3, NX, NY, NZ), F32)
    params = pltpu.CompilerParams(vmem_limit_bytes=4 << 20)

    ex, hx, px, cx, fx, strip_c, strip_d, slab_a, slab_b = pl.pallas_call(
        load_and_pack, out_shape=(field, field, field, ints, fill, strip, strip, slab1, slab1),
        in_specs=[hbm] * 6 + [smem] * 4, out_specs=(vmem,) * 9,
        scratch_shapes=[pltpu.SemaphoreType.DMA((6,))], compiler_params=params, name="load_and_pack",
    )(*cells, *tables)
    row_c = swapped(strip_c, "gy", 0)
    row_d = swapped(strip_d, "gy", 1)
    got1_b = swapped(slab_b, "gx", 1)
    got1_a = swapped(slab_a, "gx", 0)
    ex, hx, px, cx, fx, w, edge_a, edge_b = pl.pallas_call(
        first_edges, out_shape=(field, field, field, ints, fill, coef, slab2, slab2),
        in_specs=[vmem] * 2 + [smem] * 5 + [vmem] * 5, out_specs=(vmem,) * 8,
        input_output_aliases={7 + k: k for k in range(5)}, compiler_params=params, name="first_edges",
    )(row_c, row_d, *tables, conformal, ex, hx, px, cx, fx)
    got2_b = swapped(edge_b, "gx", 1)
    got2_a = swapped(edge_a, "gx", 0)
    ex, hx, px, w = pl.pallas_call(
        interior, out_shape=(field, field, field, coef),
        in_specs=[vmem] * 2 + [smem] * 5 + [vmem] * 4, out_specs=(vmem,) * 4,
        input_output_aliases={7 + k: k for k in range(4)}, compiler_params=params, name="interior",
        cost_estimate=pl.CostEstimate(flops=80_000_000, bytes_accessed=20_000_000, transcendentals=0),
    )(cx, fx, *tables, conformal, ex, hx, px, w)
    outs = pl.pallas_call(
        last_edges, out_shape=(result,) * 3 + (field, field, field, ints, fill, coef),
        in_specs=[vmem] * 4 + [smem] * 5 + [vmem] * 6, out_specs=(hbm,) * 3 + (vmem,) * 6,
        input_output_aliases={9 + k: 3 + k for k in range(6)},
        scratch_shapes=[pltpu.SemaphoreType.DMA((6,))], compiler_params=params, name="last_edges",
    )(got1_a, got1_b, got2_a, got2_b, *tables, conformal, ex, hx, px, cx, fx, w)
    return outs[:3]


def solution(mesh):
    whole, cell = P(None, "gx", "gy", None), P("gx", "gy", None)
    return jax.shard_map(
        shards, mesh=mesh, in_specs=(whole,) * 3 + (cell,) * 3 + (P(),) * 5, out_specs=(whole,) * 3, check_vma=False,
    )
```

time: 142 us -> 33 us (0.23)
  other arithmetic: 56.8 us -> 0 us
  waiting for transfers between devices: 36.5 us -> 0.2 us
  local copies, waits for them, and re-layouts: 17.7 us -> 0.01 us
  Pallas kernels: 0 us -> 16.1 us
  starting transfers between devices: 28.5 us -> 15.3 us
    ppermute x10 -> x6, waiting for transfers between devices: 36.5 us -> 0.2 us  [swapped(): return lax.ppermute(value, axis, pairs)]
    unnamed x6 -> x0, other arithmetic: 32.7 us -> none
    pallas_call x0 -> x4, Pallas kernels: none -> 16.1 us  [the longest x1 8.33 us: shards(): pl.pallas_call(interior, out_shape=(field, field, field, coef), in_specs=...]
    ppermute x10 -> x6, starting transfers between devices: 28.5 us -> 15.3 us  [swapped(): return lax.ppermute(value, axis, pairs)]
    slice x53 -> x0, local copies, waits for them, and re-layouts: 12.2 us -> none  [the longest x6 7.71 us: select(): table[entry]]
    concatenate x2 -> x0, other arithmetic: 10.2 us -> none  [the longest x1 9.29 us: cell_stack(): return jnp.concatenate([efield, hfield, polar, coef], 0)]
    sub x10 -> x0, other arithmetic: 5.29 us -> none  [the longest x3 3.44 us: shards(): coef[0] * elec + coef[4:7] * curl_h(magn, y_prev, x_zero)]
    unnamed x27 -> x2, local copies, waits for them, and re-layouts: 4.93 us -> 0.01 us
  transfers between devices with their start and end apart: 10 -> 6, of which waited for: 10 -> 1; matrix products, arithmetic and copies ran while one was open for 2% -> 0% of each run, Pallas kernels for 0% -> 30%
where the time goes in v2:
time: 33 us; the launch traced here: 32.4 us
  Pallas kernels  16.1 us (49%)
  starting transfers between devices  15.3 us (46%)
  between operations  0.73 us (2%)
    ppermute x6, starting transfers between devices, swapped(): return lax.ppermute(value, axis, pairs)  15.3 us
    pallas_call x1, Pallas kernels, shards(): pl.pallas_call(interior, out_shape=(field, field, field, coef), in_specs=...  8.33 us
    pallas_call x1, Pallas kernels, shards(): pl.pallas_call(last_edges, out_shape=(result,) * 3 + (field, field, field...  3.63 us
    pallas_call x1, Pallas kernels, shards(): pl.pallas_call(load_and_pack, out_shape=(field, field, field, ints, fill,...  2.76 us
    pallas_call x1, Pallas kernels, shards(): pl.pallas_call(first_edges, out_shape=(field, field, field, ints, fill, c...  1.38 us
  transfers between devices with their start and end apart: 6, of which 1 were waited for; matrix products, arithmetic and copies ran while one was open for 0% of the time, Pallas kernels for 30%

profile of v2, /device:TPU:122, one launch (start us, length us, event | category | flops | bytes accessed | tf_op | source)
XLA Modules:
  0.0 32.4 jit_solution(366782122527204201)
XLA Ops:
  0.6 0.0 copy-start
  0.6 2.8 %load_and_pack.1 = (f32[3,21,56,128]{3,2,1,0:T(8,128)S(1)}, f32[3,21,56,128]{3,2,1,0:T(8,128)S(1)}, f32[3,21,56,128]{3,2,1,0:T(8,128)S(1)}, s32[2,21,56,128]{3,2...) custom-call(f32[3,16,32,128]{3,2,1,0:T(8,128)} %e.1, ...), custom_call_target="tpu_custom_call" | custom-call | tf_op jit(solution)/shard_map/load_and_pack/pallas_call | solution.py:430
  3.4 0.1 collective-permute-start.2
  3.5 2.5 %collective-permute-start.3 = (f32[6,16,8,128]{3,2,1,0:T(8,128)S(1)}, f32[6,16,8,128]{3,2,1,0:T(8,128)S(1)}, u32[]{:S(2)}, u32[]{:S(2)}) collective-permute-start(f32[6,16,8,128]{3,2,1,0:T(8,128)S(1)} %get-tuple-element.30), channel_id=1, source_target_pairs={{1,2},{2,1},{3,4},{4,3},{5,6},{6,5},{9,10},{10,9},{11,12},{12,11},... | collective-permute-start | bytes 1179656 | tf_op jit(solution)/shard_map/ppermute | solution.py:26
  6.1 0.8 %collective-permute-start = (f32[18,32,128]{2,1,0:T(8,128)S(1)}, f32[18,32,128]{2,1,0:T(8,128)S(1)}, u32[]{:S(2)}, u32[]{:S(2)}) collective-permute-start(f32[18,32,128]{2,1,0:T(8,128)S(1)} %get-tuple-element.27), channel_id=1, source_target_pairs={{0,8},{8,0},{16,24},{24,16},{32,40},{40,32},{48,56},{56,48},{64,72... | collective-permute-start | bytes 884744 | tf_op jit(solution)/shard_map/ppermute | solution.py:26
  6.9 5.5 %collective-permute-start.1 = (f32[18,32,128]{2,1,0:T(8,128)S(1)}, f32[18,32,128]{2,1,0:T(8,128)S(1)}, u32[]{:S(2)}, u32[]{:S(2)}) collective-permute-start(f32[18,32,128]{2,1,0:T(8,128)S(1)} %get-tuple-element.28), channel_id=1, source_target_pairs={{8,16},{16,8},{24,32},{32,24},{40,48},{48,40},{56,64},{64,56},{72,... | collective-permute-start | bytes 884744 | tf_op jit(solution)/shard_map/ppermute | solution.py:26
  12.4 0.0 collective-permute-done.2.row_c
  12.4 0.2 collective-permute-done.3.row_d
  12.6 0.0 copy-done
  12.6 1.4 %first_edges.1 = (f32[3,21,56,128]{3,2,1,0:T(8,128)S(1)}, f32[3,21,56,128]{3,2,1,0:T(8,128)S(1)}, f32[3,21,56,128]{3,2,1,0:T(8,128)S(1)}, s32[2,21,56,128]{3,2,1...) custom-call(f32[6,16,8,128]{3,2,1,0:T(8,128)S(1)} %collective-permut, ...), custom_call_target="tpu_custom_call", output_to_operand_aliasing={{0}: (7, {}), {1}: (8, {}), {2}: (9, {}), {3}: (10, {}), {4... | custom-call | tf_op jit(solution)/shard_map/first_edges/pallas_call | solution.py:439
  14.0 0.8 %collective-permute-start.4 = (f32[464,128]{1,0:T(8,128)S(1)}, f32[464,128]{1,0:T(8,128)S(1)}, u32[]{:S(2)}, u32[]{:S(2)}) collective-permute-start(f32[464,128]{1,0:T(8,128)S(1)} %get-tuple-element.36), channel_id=1, source_target_pairs={{0,8},{8,0},{16,24},{24,16},{32,40},{40,32},{48,56},{56,48},{64,72... | collective-permute-start | bytes 712712 | tf_op jit(solution)/shard_map/ppermute | solution.py:26
  14.8 5.5 %collective-permute-start.5 = (f32[464,128]{1,0:T(8,128)S(1)}, f32[464,128]{1,0:T(8,128)S(1)}, u32[]{:S(2)}, u32[]{:S(2)}) collective-permute-start(f32[464,128]{1,0:T(8,128)S(1)} %get-tuple-element.37), channel_id=1, source_target_pairs={{8,16},{16,8},{24,32},{32,24},{40,48},{48,40},{56,64},{64,56},{72,... | collective-permute-start | bytes 712712 | tf_op jit(solution)/shard_map/ppermute | solution.py:26
  20.4 8.3 %interior.1 = (f32[3,21,56,128]{3,2,1,0:T(8,128)S(1)}, f32[3,21,56,128]{3,2,1,0:T(8,128)S(1)}, f32[3,21,56,128]{3,2,1,0:T(8,128)S(1)}, f32[7,21,56,128]{3,2,1,0:T(8,128)S(1)}) custom-call(s32[2,21,56,128]{3,2,1,0:T(8,128)S(1)} %get-tuple-element.38.cx.refs_3_, ...), custom_call_target="tpu_custom_call", output_to_operand_aliasing={{0}: (7, {}), {1}: (8, {}), {2}: (9, {}), {3}: (10, {})} | custom-call | flops 80000000 | bytes 20000000 | tf_op jit(solution)/shard_map/interior/pallas_call | solution.py:446
  28.7 0.0 collective-permute-done.got1_a
  28.7 0.0 collective-permute-done.1.got1_b
  28.7 0.0 collective-permute-done.4.got2_a
  28.7 0.0 collective-permute-done.5.got2_b
  28.7 3.6 %last_edges.1 = (f32[3,16,32,128]{3,2,1,0:T(8,128)}, f32[3,16,32,128]{3,2,1,0:T(8,128)}, f32[3,16,32,128]{3,2,1,0:T(8,128)}, f32[3,21,56,128]{3,2,1,0:T(8,128)S(...) custom-call(f32[18,32,128]{2,1,0:T(8,128)S(1)} %collective-permute-d, ...), custom_call_target="tpu_custom_call", output_to_operand_aliasing={{3}: (9, {}), {4}: (10, {}), {5}: (11, {}), {6}: (12, {}), ... | custom-call | tf_op jit(solution)/shard_map/last_edges/pallas_call | solution.py:452
Async XLA Ops:
  0.6 12.0 %copy-start = (f32[8,3]{0,1:T(4,128)S(1)}, f32[8,3]{0,1:T(4,128)}, u32[]{:S(2)}) copy-start(f32[8,3]{0,1:T(4,128)} %param.21) | copy-start | bytes 292
  3.4 9.0 %collective-permute-start.2 = (f32[6,16,8,128]{3,2,1,0:T(8,128)S(1)}, f32[6,16,8,128]{3,2,1,0:T(8,128)S(1)}, u32[]{:S(2)}, u32[]{:S(2)}) collective-permute-start(f32[6,16,8,128]{3,2,1,0:T(8,128)S(1)} %get-tuple-element.29), channel_id=1, source_target_pairs={{0,1},{1,0},{2,3},{3,2},{4,5},{5,4},{6,7},{7,6},{8,9},{9,8},{10,11... | collective-permute-start | bytes 1179656 | tf_op jit(solution)/shard_map/ppermute | solution.py:26
  3.5 9.1 %collective-permute-start.3 = (f32[6,16,8,128]{3,2,1,0:T(8,128)S(1)}, f32[6,16,8,128]{3,2,1,0:T(8,128)S(1)}, u32[]{:S(2)}, u32[]{:S(2)}) collective-permute-start(f32[6,16,8,128]{3,2,1,0:T(8,128)S(1)} %get-tuple-element.30), channel_id=1, source_target_pairs={{1,2},{2,1},{3,4},{4,3},{5,6},{6,5},{9,10},{10,9},{11,12},{12,11},... | collective-permute-start | bytes 1179656 | tf_op jit(solution)/shard_map/ppermute | solution.py:26
  6.1 22.6 %collective-permute-start = (f32[18,32,128]{2,1,0:T(8,128)S(1)}, f32[18,32,128]{2,1,0:T(8,128)S(1)}, u32[]{:S(2)}, u32[]{:S(2)}) collective-permute-start(f32[18,32,128]{2,1,0:T(8,128)S(1)} %get-tuple-element.27), channel_id=1, source_target_pairs={{0,8},{8,0},{16,24},{24,16},{32,40},{40,32},{48,56},{56,48},{64,72... | collective-permute-start | bytes 884744 | tf_op jit(solution)/shard_map/ppermute | solution.py:26
  6.9 21.8 %collective-permute-start.1 = (f32[18,32,128]{2,1,0:T(8,128)S(1)}, f32[18,32,128]{2,1,0:T(8,128)S(1)}, u32[]{:S(2)}, u32[]{:S(2)}) collective-permute-start(f32[18,32,128]{2,1,0:T(8,128)S(1)} %get-tuple-element.28), channel_id=1, source_target_pairs={{8,16},{16,8},{24,32},{32,24},{40,48},{48,40},{56,64},{64,56},{72,... | collective-permute-start | bytes 884744 | tf_op jit(solution)/shard_map/ppermute | solution.py:26
  14.0 14.7 %collective-permute-start.4 = (f32[464,128]{1,0:T(8,128)S(1)}, f32[464,128]{1,0:T(8,128)S(1)}, u32[]{:S(2)}, u32[]{:S(2)}) collective-permute-start(f32[464,128]{1,0:T(8,128)S(1)} %get-tuple-element.36), channel_id=1, source_target_pairs={{0,8},{8,0},{16,24},{24,16},{32,40},{40,32},{48,56},{56,48},{64,72... | collective-permute-start | bytes 712712 | tf_op jit(solution)/shard_map/ppermute | solution.py:26
  14.8 13.9 %collective-permute-start.5 = (f32[464,128]{1,0:T(8,128)S(1)}, f32[464,128]{1,0:T(8,128)S(1)}, u32[]{:S(2)}, u32[]{:S(2)}) collective-permute-start(f32[464,128]{1,0:T(8,128)S(1)} %get-tuple-element.37), channel_id=1, source_target_pairs={{8,16},{16,8},{24,32},{32,24},{40,48},{48,40},{56,64},{64,56},{72,... | collective-permute-start | bytes 712712 | tf_op jit(solution)/shard_map/ppermute | solution.py:26

commit v3 on v2

v3 whole, which is shorter than its diff:
```python
import jax
import jax.numpy as jnp
from jax import lax
from jax.experimental import pallas as pl
from jax.experimental.pallas import tpu as pltpu
from jax.sharding import PartitionSpec as P

DT = 0.55
F32 = jnp.float32

NX, NY, NZ = 16, 32, 128
LOW, HIGH = 3, 2
R0, RH, RE = 8, 8 + NY, 16 + NY
EXT = (NX + LOW + HIGH, RE + 8, NZ)
TILES = (RE - R0) // 8
OWN, HALO = range(TILES - 1), range(TILES - 1, TILES)
MSG1, MSG2 = 18, 8
MSG2_ROWS = MSG2 * (RE - R0) + MSG1 * 8

ORDER = (("e", 0), ("e", 1), ("e", 2), ("h", 0), ("h", 1), ("h", 2), ("p", 0), ("p", 1), ("p", 2), ("f", 0), ("c", 0), ("c", 1))


def swapped(value, axis, first):
    pairs = []
    for low in range(first, lax.axis_size(axis) - 1, 2):
        pairs += [(low, low + 1), (low + 1, low)]
    return lax.ppermute(value, axis, pairs)


def tile_iota(dim):
    return lax.broadcasted_iota(jnp.int32, (8, NZ), dim)


def make_tables(perm, cond, stre, rlx, conf, tab):
    for m in range(3):
        tau = jnp.full((8, NZ), rlx[m], F32)
        inv = 1.0 / (2.0 * tau + DT)
        tab[5 * m] = jnp.full((8, NZ), perm[m], F32)
        tab[5 * m + 1] = jnp.full((8, NZ), cond[m] * (DT / 2), F32)
        tab[5 * m + 2] = (2.0 * tau - DT) * inv
        tab[5 * m + 3] = jnp.full((8, NZ), stre[m], F32) * (2.0 * DT) * inv
        tab[5 * m + 4] = 2.0 * DT * inv
    lane = tile_iota(1)
    for c in range(3):
        table = jnp.zeros((8, NZ), F32)
        for v in range(8):
            table = jnp.where(lane == v, conf[c, v], table)
        tab[15 + c] = table


def pick(tab, m, i):
    return jnp.where(m == 0, tab[i], jnp.where(m == 1, tab[5 + i], tab[10 + i]))


class Block:
    def __init__(self, ex, hx, px, cx, fx, w=None):
        self.e, self.h, self.p, self.c, self.f, self.w = ex, hx, px, cx, fx, w

    def masks(self):
        gy = lax.axis_index("gy")
        row = tile_iota(0)
        out = ((row < 4) & (gy == lax.axis_size("gy") - 1)) | ((row >= 4) & (gy == 0))
        self.row_in = jnp.where(out, 0.0, 1.0).astype(F32)
        lane = tile_iota(1)
        self.last, self.first = lane == NZ - 1, lane == 0

    def plane_in(self, x):
        if not isinstance(x, int) or 0 <= x < NX:
            return None
        gx = lax.axis_index("gx")
        out = gx == 0 if x < 0 else gx == lax.axis_size("gx") - 1
        return jnp.where(out, 0.0, 1.0).astype(F32)

    def zf(self, a):
        return jnp.where(self.last, 0.0, pltpu.roll(a, NZ - 1, 1))

    def zb(self, a):
        return jnp.where(self.first, 0.0, pltpu.roll(a, 1, 1))

    def coef(self, x, tab, tiles):
        i = x + LOW
        inside = self.plane_in(x)
        for t in tiles:
            r = slice(R0 + 8 * t, R0 + 8 * t + 8)
            m, v, f = self.c[0, i, r], self.c[1, i, r], self.f[0, i, r]
            pe, s, kp, bp, omk = (pick(tab, m, k) for k in range(5))
            eps = pe * (1.0 + f)
            inv = 1.0 / (eps + s)
            self.w[0, i, r] = (eps - s) * inv - inv * bp
            self.w[1, i, r] = inv * omk
            self.w[2, i, r] = kp
            self.w[3, i, r] = bp
            scale = inv * DT if inside is None else inv * (DT * inside)
            if t == TILES - 1:
                scale = scale * self.row_in
            for c in range(3):
                self.w[4 + c, i, r] = scale * jnp.take_along_axis(tab[15 + c], v, axis=1)

    def take_tiles(self, below, part, rows):
        d1, d2 = (LOW - 1, LOW - 2) if below else (LOW + NX, LOW + NX + 1)
        for c in range(3):
            self.e[c, d1, rows] = part(c)
            self.p[c, d1, rows] = part(3 + c)
            self.p[c, d2, rows] = part(12 + c)
            if below:
                self.h[c, d1, rows] = part(15 + c)
        for k, i in ((6, d1), (9, d2)):
            self.c[0, i, rows] = part(k).astype(jnp.int32)
            self.c[1, i, rows] = part(k + 1).astype(jnp.int32)
            self.f[0, i, rows] = part(k + 2)

    def h_plane(self, x):
        i = x + LOW
        e, h = self.e, self.h
        inside = self.plane_in(x)
        for t in range(TILES):
            a = R0 + 8 * t
            r, up = slice(a, a + 8), slice(a + 1, a + 9)
            e0, e1, e2 = e[0, i, r], e[1, i, r], e[2, i, r]
            m = DT if inside is None else DT * inside
            if t == TILES - 1:
                m = self.row_in * m
            h0 = h[0, i, r] - m * ((e[2, i, up] - e2) - (self.zf(e1) - e1))
            h1 = h[1, i, r] - m * ((self.zf(e0) - e0) - (e[2, i + 1, r] - e2))
            h2 = h[2, i, r] - m * ((e[1, i + 1, r] - e1) - (e[0, i, up] - e0))
            h[0, i, r], h[1, i, r], h[2, i, r] = h0, h1, h2
        h[0, i, R0 - 1:R0] = h0[7:8]
        h[2, i, R0 - 1:R0] = h2[7:8]

    def e_plane(self, x, tiles=range(TILES)):
        i = x + LOW
        e, h, p, w = self.e, self.h, self.p, self.w
        for t in tiles:
            a = R0 + 8 * t
            r, down = slice(a, a + 8), slice(a - 1, a + 7)
            h0, h1, h2 = h[0, i, r], h[1, i, r], h[2, i, r]
            curl = (
                (h2 - h[2, i, down]) - (h1 - self.zb(h1)),
                (h0 - self.zb(h0)) - (h2 - h[2, i - 1, r]),
                (h1 - h[1, i - 1, r]) - (h0 - h[0, i, down]),
            )
            w0, w1, w2, w3 = (w[k, i, r] for k in range(4))
            for c in range(3):
                ec, pc = e[c, i, r], p[c, i, r]
                new = w0 * ec + w1 * pc + w[4 + c, i, r] * curl[c]
                e[c, i, r] = new
                p[c, i, r] = w2 * pc + w3 * ec
                if t == 0 and c != 1 and len(tiles) == TILES:
                    e[c, i, RE:RE + 1] = new[0:1]

    def sweep(self, h_planes, e_planes, tiles=range(TILES)):
        for x in range(min(h_planes[0], e_planes[0]), max(h_planes[1], e_planes[1]) + 1):
            if h_planes[0] <= x <= h_planes[1]:
                self.h_plane(x)
            if e_planes[0] <= x <= e_planes[1]:
                self.e_plane(x, tiles)


def for_sides(take, from_a, from_b):
    odd = lax.axis_index("gx") % 2

    @pl.when(odd == 0)
    def _():
        take(*from_a, False)
        take(*from_b, True)

    @pl.when(odd == 1)
    def _():
        take(*from_b, False)
        take(*from_a, True)


def copy_all(pairs, sems):
    copies = [pltpu.make_async_copy(a, b, sems.at[k]) for k, (a, b) in enumerate(pairs)]
    for copy in copies:
        copy.start()
    return copies


def load_and_pack(e, h, p, mat, via, fill, perm, cond, stre, rlx, conf, ex, hx, px, cx, fx, tab, out_c, out_d, out_a, out_b, *scratch):
    smalls, sems = scratch[:5], scratch[5]
    own = pl.ds(LOW, NX)
    copies = []
    for at, n in ((0, 8), (NY - 8, 8), (8, NY - 16)):
        there, here = pl.ds(at, n), pl.ds(R0 + at, n)
        pairs = [(a.at[:, :, there], b.at[:, own, here]) for a, b in ((e, ex), (h, hx), (p, px))]
        pairs += [(a.at[:, there], b.at[k, own, here]) for a, b, k in ((mat, cx, 0), (via, cx, 1), (fill, fx, 0))]
        copies += copy_all(pairs, sems.at[pl.ds(len(copies), 6)])
    few = copy_all(zip((perm, cond, stre, rlx, conf), smalls), sems.at[pl.ds(18, 5)])
    for copy in few:
        copy.wait()
    make_tables(*smalls, tab)
    for copy in copies[:12]:
        copy.wait()
    refs = {"e": ex, "h": hx, "p": px, "c": cx, "f": fx}
    low = tile_iota(0) < 4
    gy_odd, gx_odd = lax.axis_index("gy") % 2, lax.axis_index("gx") % 2

    def strip(x, r, out, upward):
        tiles = [refs[n][c, x + LOW, r:r + 8].astype(F32) for n, c in ORDER]
        for k in range(6):
            a, b = tiles[2 * k], tiles[2 * k + 1]
            if upward:
                out[k, x] = jnp.where(low, pltpu.roll(a, 4, 0), b)
            else:
                out[k, x] = jnp.where(low, a, pltpu.roll(b, 4, 0))

    def strips(up, down):
        def body(x, _):
            strip(x, RH - 8, up, True)
            strip(x, R0, down, False)
            return 0

        lax.fori_loop(0, NX, body, 0, unroll=2)

    @pl.when(gy_odd == 0)
    def _():
        strips(out_c, out_d)

    @pl.when(gy_odd == 1)
    def _():
        strips(out_d, out_c)

    for copy in copies[12:]:
        copy.wait()
    own_rows = slice(R0, RH)

    def slab(out, d1, d2):
        for c in range(3):
            out[c] = ex[c, d1, own_rows]
            out[3 + c] = px[c, d1, own_rows]
            out[15 + c] = hx[c, d1, own_rows]
        for k, i in ((6, d1), (9, d2)):
            out[k] = cx[0, i, own_rows].astype(F32)
            out[k + 1] = cx[1, i, own_rows].astype(F32)
            out[k + 2] = fx[0, i, own_rows]
        for t in range(NY // 8):
            r = slice(R0 + 8 * t, R0 + 8 * t + 8)
            m = cx[0, d2, r]
            kp, bp = pick(tab, m, 2), pick(tab, m, 3)
            for c in range(3):
                out[12 + c, 8 * t:8 * t + 8] = kp * px[c, d2, r] + bp * ex[c, d2, r]

    @pl.when(gx_odd == 0)
    def _():
        slab(out_a, LOW + NX - 1, LOW + NX - 2)
        slab(out_b, LOW, LOW + 1)

    @pl.when(gx_odd == 1)
    def _():
        slab(out_b, LOW + NX - 1, LOW + NX - 2)
        slab(out_a, LOW, LOW + 1)


def own_coefs(cx, fx, tab, w):
    b = Block(None, None, None, cx, fx, w)

    def body(x, _):
        b.coef(x, tab, OWN)
        return 0

    lax.fori_loop(0, NX, body, 0, unroll=2)


def first_edges(row_c, row_d, tab, *refs):
    ex, hx, px, cx, fx, w, out_a, out_b = refs[6:]
    b = Block(ex, hx, px, cx, fx, w)
    b.masks()
    named = {"e": ex, "h": hx, "p": px, "c": cx, "f": fx}
    low = tile_iota(0) < 4
    gy_odd, gx_odd = lax.axis_index("gy") % 2, lax.axis_index("gx") % 2

    def rows_body(x, above_ref, below_ref):
        for k in range(6):
            above, below = above_ref[k, x], below_ref[k, x]
            both = (jnp.where(low, above, pltpu.roll(below, 4, 0)), jnp.where(low, pltpu.roll(above, 4, 0), below))
            for (n, c), tile in zip(ORDER[2 * k:2 * k + 2], both):
                named[n][c, x + LOW, RH:RE] = tile.astype(jnp.int32) if n == "c" else tile
        for c in (0, 2):
            ex[c, x + LOW, RE:RE + 1] = ex[c, x + LOW, R0:R0 + 1]
            hx[c, x + LOW, R0 - 1:R0] = hx[c, x + LOW, RE - 1:RE]

    def all_rows(above_ref, below_ref):
        def body(x, _):
            rows_body(x, above_ref, below_ref)
            return 0

        lax.fori_loop(0, NX, body, 0, unroll=2)

    @pl.when(gy_odd == 0)
    def _():
        all_rows(row_c, row_d)

    @pl.when(gy_odd == 1)
    def _():
        all_rows(row_d, row_c)

    for x in (1, 2, NX - 3, NX - 2):
        b.coef(x, tab, HALO)
    b.h_plane(0)
    for x in (1, 2):
        b.h_plane(x)
        b.e_plane(x)
    b.h_plane(1)
    b.h_plane(NX - 4)
    for x in (NX - 3, NX - 2):
        b.h_plane(x)
        b.e_plane(x)
    b.h_plane(NX - 3)

    n = RE - R0

    def message(out, upward):
        d1, d2, d3 = (LOW + NX - 1, LOW + NX - 2, LOW + NX - 3) if upward else (LOW, LOW + 1, None)
        if upward:
            planes = [(hx, c, d2) for c in range(3)] + [(ex, c, d2) for c in range(3)] + [(hx, c, d3) for c in (1, 2)]
        else:
            planes = [(hx, c, d1) for c in range(3)] + [(hx, c, d2) for c in range(3)] + [(ex, c, d2) for c in (1, 2)]
        for k, (ref, c, i) in enumerate(planes):
            out[n * k:n * k + n] = ref[c, i, R0:RE]
        tiles = [(ex, c, d1) for c in range(3)] + [(px, c, d1) for c in range(3)]
        for i in (d1, d2):
            tiles += [(cx, 0, i), (cx, 1, i), (fx, 0, i)]
        tiles += [(px, c, d2) for c in range(3)] + [(hx, c, d1) for c in range(3)]
        for k, (ref, c, i) in enumerate(tiles):
            at = MSG2 * n + 8 * k
            out[at:at + 8] = ref[c, i, RH:RE].astype(F32)

    @pl.when(gx_odd == 0)
    def _():
        message(out_a, True)
        message(out_b, False)

    @pl.when(gx_odd == 1)
    def _():
        message(out_b, True)
        message(out_a, False)


def interior(cx, fx, tab, *refs):
    ex, hx, px, w = refs[4:]
    b = Block(ex, hx, px, cx, fx, w)
    b.masks()
    for x in (0, *range(3, NX - 3), NX - 1):
        b.coef(x, tab, HALO)
    b.sweep((3, NX - 5), (3, NX - 4))
    b.sweep((2, NX - 4), (2, NX - 3))
    b.sweep((2, NX - 4), (3, NX - 4))
    b.sweep((3, NX - 5), (4, NX - 5), OWN)


def neighbour_cells(got1_a, got1_b, tab, *refs):
    ex, hx, px, cx, fx, w = refs[6:]
    b = Block(ex, hx, px, cx, fx, w)

    def take(m1, below):
        b.take_tiles(below, lambda k: m1[k], slice(R0, RH))

    for_sides(take, (got1_a,), (got1_b,))
    for x in (-2, -1, NX, NX + 1):
        b.coef(x, tab, OWN)


def last_edges(got2_a, got2_b, tab, *refs):
    e_out, h_out, p_out, ex, hx, px, cx, fx, w, sems = refs[6:]
    b = Block(ex, hx, px, cx, fx, w)
    b.masks()
    rows = pl.ds(R0, NY)
    done = []

    def store(first, count):
        pairs = []
        for src, dst in ((ex, e_out), (hx, h_out), (px, p_out)):
            pairs.append((src.at[:, pl.ds(LOW + first, count), rows], dst.at[:, pl.ds(first, count)]))
        done.extend(copy_all(pairs, sems.at[pl.ds(len(done), 3)]))

    store(4, NX - 8)
    n = RE - R0

    def take(m2, below):
        at = MSG2 * n
        b.take_tiles(below, lambda k: m2[at + 8 * k:at + 8 * k + 8], slice(RH, RE))
        d1, d2, d3 = (LOW - 1, LOW - 2, LOW - 3) if below else (LOW + NX, LOW + NX + 1, None)
        if below:
            planes = [(hx, c, d2) for c in range(3)] + [(ex, c, d2) for c in range(3)] + [(hx, c, d3) for c in (1, 2)]
        else:
            planes = [(hx, c, d1) for c in range(3)] + [(hx, c, d2) for c in range(3)] + [(ex, c, d2) for c in (1, 2)]
        for k, (ref, c, i) in enumerate(planes):
            ref[c, i, R0:RE] = m2[n * k:n * k + n]
        for i in (d1, d2):
            for c in (0, 2):
                ex[c, i, RE:RE + 1] = ex[c, i, R0:R0 + 1]
                hx[c, i, R0 - 1:R0] = hx[c, i, RE - 1:RE]

    for_sides(take, (got2_a,), (got2_b,))
    for x in (-2, -1, NX, NX + 1):
        b.coef(x, tab, HALO)
    b.sweep((-1, -1), (-1, 0))
    b.sweep((-2, 0), (-2, 1))
    b.sweep((-2, 1), (-1, 2))
    b.sweep((-1, 2), (0, 3), OWN)
    store(0, 4)
    b.sweep((NX - 1, NX - 1), (NX - 1, NX))
    b.sweep((NX - 2, NX), (NX - 2, NX + 1))
    b.sweep((NX - 3, NX), (NX - 3, NX))
    b.sweep((NX - 4, NX - 1), (NX - 4, NX - 1), OWN)
    store(NX - 4, 4)
    for copy in done:
        copy.wait()


def shards(efield, hfield, polar, material_map, via_index, fill_fraction, permittivity, conductivity, debye_strength, relax_time, conformal):
    vmem = pl.BlockSpec(memory_space=pltpu.VMEM)
    hbm = pl.BlockSpec(memory_space=pltpu.HBM)
    conformal = conformal.T
    cells = (efield, hfield, polar, material_map, via_index, fill_fraction)
    cells = tuple(pltpu.with_memory_space_constraint(a, pltpu.HBM) for a in cells)
    tables = (permittivity, conductivity, debye_strength, relax_time, conformal)
    tables = tuple(pltpu.with_memory_space_constraint(a, pltpu.HBM) for a in tables)
    shape = jax.ShapeDtypeStruct
    field, slab1 = shape((3,) + EXT, F32), shape((MSG1, NY, NZ), F32)
    slab2, strip = shape((MSG2_ROWS, NZ), F32), shape((6, NX, 8, NZ), F32)
    ints, fill, coef = shape((2,) + EXT, jnp.int32), shape((1,) + EXT, F32), shape((7,) + EXT, F32)
    result = shape((3, NX, NY, NZ), F32)
    params = pltpu.CompilerParams(vmem_limit_bytes=4 << 20)

    ex, hx, px, cx, fx, tab, strip_c, strip_d, slab_a, slab_b = pl.pallas_call(
        load_and_pack, out_shape=(field, field, field, ints, fill, shape((18, 8, NZ), F32), strip, strip, slab1, slab1),
        in_specs=[hbm] * 11, out_specs=(vmem,) * 10,
        scratch_shapes=[pltpu.SMEM((3,), F32)] * 4 + [pltpu.SMEM((3, 8), F32), pltpu.SemaphoreType.DMA((23,))],
        compiler_params=params, name="load_and_pack",
    )(*cells, *tables)
    row_c = swapped(strip_c, "gy", 0)
    row_d = swapped(strip_d, "gy", 1)
    got1_a = swapped(slab_a, "gx", 0)
    got1_b = swapped(slab_b, "gx", 1)
    w = pl.pallas_call(
        own_coefs, out_shape=coef, in_specs=[vmem] * 3, out_specs=vmem, compiler_params=params, name="own_coefs",
        cost_estimate=pl.CostEstimate(flops=10_000_000, bytes_accessed=4_000_000, transcendentals=0),
    )(cx, fx, tab)
    ex, hx, px, cx, fx, w, send_a, send_b = pl.pallas_call(
        first_edges, out_shape=(field, field, field, ints, fill, coef, slab2, slab2),
        in_specs=[vmem] * 9, out_specs=(vmem,) * 8,
        input_output_aliases={3 + k: k for k in range(6)}, compiler_params=params, name="first_edges",
    )(row_c, row_d, tab, ex, hx, px, cx, fx, w)
    got2_a = swapped(send_a, "gx", 0)
    got2_b = swapped(send_b, "gx", 1)
    ex, hx, px, w = pl.pallas_call(
        interior, out_shape=(field, field, field, coef),
        in_specs=[vmem] * 7, out_specs=(vmem,) * 4,
        input_output_aliases={3 + k: k for k in range(4)}, compiler_params=params, name="interior",
        cost_estimate=pl.CostEstimate(flops=80_000_000, bytes_accessed=20_000_000, transcendentals=0),
    )(cx, fx, tab, ex, hx, px, w)
    state = (ex, hx, px, cx, fx, w)
    shapes = (field, field, field, ints, fill, coef)
    state = pl.pallas_call(
        neighbour_cells, out_shape=shapes, in_specs=[vmem] * 9, out_specs=(vmem,) * 6,
        input_output_aliases={3 + k: k for k in range(6)}, compiler_params=params, name="neighbour_cells",
    )(got1_a, got1_b, tab, *state)
    outs = pl.pallas_call(
        last_edges, out_shape=(result,) * 3 + shapes, in_specs=[vmem] * 9, out_specs=(hbm,) * 3 + (vmem,) * 6,
        input_output_aliases={3 + k: 3 + k for k in range(6)},
        scratch_shapes=[pltpu.SemaphoreType.DMA((9,))], compiler_params=params, name="last_edges",
    )(got2_a, got2_b, tab, *state)
    return outs[:3]


def solution(mesh):
    whole, cell = P(None, "gx", "gy", None), P("gx", "gy", None)

    return jax.shard_map(
        shards, mesh=mesh, in_specs=(whole,) * 3 + (cell,) * 3 + (P(),) * 5, out_specs=(whole,) * 3, check_vma=False,
    )
```

time: 33 us -> 30.6 us (0.927)
  the two profiles are of different devices: /device:TPU:122 before, /device:TPU:130 now
where the time goes in v3:
time: 30.6 us; the launch traced here: 30.4 us
  starting transfers between devices  13.3 us (43%)
  Pallas kernels  10.3 us (34%)
  waiting for transfers between devices  6.18 us (20%)
  between operations  0.72 us (2%)
    ppermute x6, starting transfers between devices, swapped(): return lax.ppermute(value, axis, pairs)  13.3 us
    ppermute x6, waiting for transfers between devices, swapped(): return lax.ppermute(value, axis, pairs)  6.18 us
    pallas_call x1, Pallas kernels, shards(): pl.pallas_call(interior, out_shape=(field, field, field, coef), in_specs=...  3.57 us
    pallas_call x1, Pallas kernels, shards(): pl.pallas_call(last_edges, out_shape=(result,) * 3 + shapes, in_specs=[vm...  2.73 us
    pallas_call x1, Pallas kernels, shards(): pl.pallas_call(load_and_pack, out_shape=(field, field, field, ints, fill,...  2.24 us
    pallas_call x1, Pallas kernels, shards(): pl.pallas_call(own_coefs, out_shape=coef, in_specs=[vmem] * 3, out_specs=...  0.95 us
  transfers between devices with their start and end apart: 6, of which 3 were waited for; matrix products, arithmetic and copies ran while one was open for 0% of the time, Pallas kernels for 17%

profile of v3, /device:TPU:130, one launch (start us, length us, event | category | flops | bytes accessed | tf_op | source)
XLA Modules:
  0.0 30.4 jit_solution(12671748466943822965)
XLA Ops:
  0.6 2.2 %load_and_pack.1 = (f32[3,21,56,128]{3,2,1,0:T(8,128)S(1)}, f32[3,21,56,128]{3,2,1,0:T(8,128)S(1)}, f32[3,21,56,128]{3,2,1,0:T(8,128)S(1)}, s32[2,21,56,128]{3,2...) custom-call(f32[3,16,32,128]{3,2,1,0:T(8,128)} %e.1, ...), custom_call_target="tpu_custom_call" | custom-call | tf_op jit(solution)/shard_map/load_and_pack/pallas_call | solution.py:427
  2.9 0.1 collective-permute-start
  3.0 2.5 %collective-permute-start.1 = (f32[6,16,8,128]{3,2,1,0:T(8,128)S(1)}, f32[6,16,8,128]{3,2,1,0:T(8,128)S(1)}, u32[]{:S(2)}, u32[]{:S(2)}) collective-permute-start(f32[6,16,8,128]{3,2,1,0:T(8,128)S(1)} %get-tuple-element.35), channel_id=1, source_target_pairs={{1,2},{2,1},{3,4},{4,3},{5,6},{6,5},{9,10},{10,9},{11,12},{12,11},... | collective-permute-start | bytes 1179656 | tf_op jit(solution)/shard_map/ppermute | solution.py:27
  5.5 1.7 %collective-permute-start.4 = (f32[18,32,128]{2,1,0:T(8,128)S(1)}, f32[18,32,128]{2,1,0:T(8,128)S(1)}, u32[]{:S(2)}, u32[]{:S(2)}) collective-permute-start(f32[18,32,128]{2,1,0:T(8,128)S(1)} %get-tuple-element.44), channel_id=1, source_target_pairs={{0,8},{8,0},{16,24},{24,16},{32,40},{40,32},{48,56},{56,48},{64,72... | collective-permute-start | bytes 884744 | tf_op jit(solution)/shard_map/ppermute | solution.py:27
  7.2 3.6 %collective-permute-start.5 = (f32[18,32,128]{2,1,0:T(8,128)S(1)}, f32[18,32,128]{2,1,0:T(8,128)S(1)}, u32[]{:S(2)}, u32[]{:S(2)}) collective-permute-start(f32[18,32,128]{2,1,0:T(8,128)S(1)} %get-tuple-element.45), channel_id=1, source_target_pairs={{8,16},{16,8},{24,32},{32,24},{40,48},{48,40},{56,64},{64,56},{72,... | collective-permute-start | bytes 884744 | tf_op jit(solution)/shard_map/ppermute | solution.py:27
  10.8 1.0 %own_coefs.1.refs_5_ = f32[7,21,56,128]{3,2,1,0:T(8,128)S(1)} custom-call(s32[2,21,56,128]{3,2,1,0:T(8,128)S(1)} %get-tuple-element.40.cx.refs_3_, f32[1,21,56,128]{3,2,1,0:T(8,128)S(1)} %get-tuple-element.41.fx.refs_4_, f32[18,8,128]{2,1,0:T(8,128)S(1)} %get-tuple-element.36.tab), custom_call_target="tpu_custom_call" | custom-call | flops 10000000 | bytes 4000000 | tf_op jit(solution)/shard_map/own_coefs/pallas_call | solution.py:437
  11.8 0.0 collective-permute-done.row_c
  11.8 0.3 collective-permute-done.1.row_d
  12.1 0.6 %first_edges.1 = (f32[3,21,56,128]{3,2,1,0:T(8,128)S(1)}, f32[3,21,56,128]{3,2,1,0:T(8,128)S(1)}, f32[3,21,56,128]{3,2,1,0:T(8,128)S(1)}, s32[2,21,56,128]{3,2,1...) custom-call(f32[6,16,8,128]{3,2,1,0:T(8,128)S(1)} %collective-permut, ...), custom_call_target="tpu_custom_call", output_to_operand_aliasing={{0}: (3, {}), {1}: (4, {}), {2}: (5, {}), {3}: (6, {}), {4}... | custom-call | tf_op jit(solution)/shard_map/first_edges/pallas_call | solution.py:441
  12.7 1.7 %collective-permute-start.2 = (f32[464,128]{1,0:T(8,128)S(1)}, f32[464,128]{1,0:T(8,128)S(1)}, u32[]{:S(2)}, u32[]{:S(2)}) collective-permute-start(f32[464,128]{1,0:T(8,128)S(1)} %get-tuple-element.42), channel_id=1, source_target_pairs={{0,8},{8,0},{16,24},{24,16},{32,40},{40,32},{48,56},{56,48},{64,72... | collective-permute-start | bytes 712712 | tf_op jit(solution)/shard_map/ppermute | solution.py:27
  14.3 3.7 %collective-permute-start.3 = (f32[464,128]{1,0:T(8,128)S(1)}, f32[464,128]{1,0:T(8,128)S(1)}, u32[]{:S(2)}, u32[]{:S(2)}) collective-permute-start(f32[464,128]{1,0:T(8,128)S(1)} %get-tuple-element.43), channel_id=1, source_target_pairs={{8,16},{16,8},{24,32},{32,24},{40,48},{48,40},{56,64},{64,56},{72,... | collective-permute-start | bytes 712712 | tf_op jit(solution)/shard_map/ppermute | solution.py:27
  18.0 3.6 %interior.1 = (f32[3,21,56,128]{3,2,1,0:T(8,128)S(1)}, f32[3,21,56,128]{3,2,1,0:T(8,128)S(1)}, f32[3,21,56,128]{3,2,1,0:T(8,128)S(1)}, f32[7,21,56,128]{3,2,1,0:T(8,128)S(1)}) custom-call(s32[2,21,56,128]{3,2,1,0:T(8,128)S(1)} %get-tuple-element.46.cx.refs_3_, ...), custom_call_target="tpu_custom_call", output_to_operand_aliasing={{0}: (3, {}), {1}: (4, {}), {2}: (5, {}), {3}: (6, {})} | custom-call | flops 80000000 | bytes 20000000 | tf_op jit(solution)/shard_map/interior/pallas_call | solution.py:448
  21.6 0.0 collective-permute-done.4.got1_a
  21.6 0.4 %collective-permute-done.5.got1_b = f32[18,32,128]{2,1,0:T(8,128)S(1)} collective-permute-done((f32[18,32,128]{2,1,0:T(8,128)S(1)}, f32[18,32,128]{2,1,0:T(8,128)S(1)}, u32[]{:S(2)}, u32[]{:S(2)}) %collective-permute-start.5) | collective-permute-done | bytes 294944 | tf_op jit(solution)/shard_map/ppermute | solution.py:27
  22.0 0.2 neighbour_cells.1
  22.2 0.0 collective-permute-done.2.got2_a
  22.2 5.5 %collective-permute-done.3.got2_b = f32[464,128]{1,0:T(8,128)S(1)} collective-permute-done((f32[464,128]{1,0:T(8,128)S(1)}, f32[464,128]{1,0:T(8,128)S(1)}, u32[]{:S(2)}, u32[]{:S(2)}) %collective-permute-start.3) | collective-permute-done | bytes 237600 | tf_op jit(solution)/shard_map/ppermute | solution.py:27
  27.7 2.7 %last_edges.1 = (f32[3,16,32,128]{3,2,1,0:T(8,128)}, f32[3,16,32,128]{3,2,1,0:T(8,128)}, f32[3,16,32,128]{3,2,1,0:T(8,128)}, f32[3,21,56,128]{3,2,1,0:T(8,128)S(...) custom-call(f32[464,128]{1,0:T(8,128)S(1)} %collective-permute-done., ...), custom_call_target="tpu_custom_call", output_to_operand_aliasing={{3}: (3, {}), {4}: (4, {}), {5}: (5, {}), {6}: (6, {}), {7}... | custom-call | tf_op jit(solution)/shard_map/last_edges/pallas_call | solution.py:460
Async XLA Ops:
  2.9 8.9 %collective-permute-start = (f32[6,16,8,128]{3,2,1,0:T(8,128)S(1)}, f32[6,16,8,128]{3,2,1,0:T(8,128)S(1)}, u32[]{:S(2)}, u32[]{:S(2)}) collective-permute-start(f32[6,16,8,128]{3,2,1,0:T(8,128)S(1)} %get-tuple-element.34), channel_id=1, source_target_pairs={{0,1},{1,0},{2,3},{3,2},{4,5},{5,4},{6,7},{7,6},{8,9},{9,8},{10,11... | collective-permute-start | bytes 1179656 | tf_op jit(solution)/shard_map/ppermute | solution.py:27
  3.0 9.1 %collective-permute-start.1 = (f32[6,16,8,128]{3,2,1,0:T(8,128)S(1)}, f32[6,16,8,128]{3,2,1,0:T(8,128)S(1)}, u32[]{:S(2)}, u32[]{:S(2)}) collective-permute-start(f32[6,16,8,128]{3,2,1,0:T(8,128)S(1)} %get-tuple-element.35), channel_id=1, source_target_pairs={{1,2},{2,1},{3,4},{4,3},{5,6},{6,5},{9,10},{10,9},{11,12},{12,11},... | collective-permute-start | bytes 1179656 | tf_op jit(solution)/shard_map/ppermute | solution.py:27
  5.5 16.1 %collective-permute-start.4 = (f32[18,32,128]{2,1,0:T(8,128)S(1)}, f32[18,32,128]{2,1,0:T(8,128)S(1)}, u32[]{:S(2)}, u32[]{:S(2)}) collective-permute-start(f32[18,32,128]{2,1,0:T(8,128)S(1)} %get-tuple-element.44), channel_id=1, source_target_pairs={{0,8},{8,0},{16,24},{24,16},{32,40},{40,32},{48,56},{56,48},{64,72... | collective-permute-start | bytes 884744 | tf_op jit(solution)/shard_map/ppermute | solution.py:27
  7.2 14.8 %collective-permute-start.5 = (f32[18,32,128]{2,1,0:T(8,128)S(1)}, f32[18,32,128]{2,1,0:T(8,128)S(1)}, u32[]{:S(2)}, u32[]{:S(2)}) collective-permute-start(f32[18,32,128]{2,1,0:T(8,128)S(1)} %get-tuple-element.45), channel_id=1, source_target_pairs={{8,16},{16,8},{24,32},{32,24},{40,48},{48,40},{56,64},{64,56},{72,... | collective-permute-start | bytes 884744 | tf_op jit(solution)/shard_map/ppermute | solution.py:27
  12.7 9.6 %collective-permute-start.2 = (f32[464,128]{1,0:T(8,128)S(1)}, f32[464,128]{1,0:T(8,128)S(1)}, u32[]{:S(2)}, u32[]{:S(2)}) collective-permute-start(f32[464,128]{1,0:T(8,128)S(1)} %get-tuple-element.42), channel_id=1, source_target_pairs={{0,8},{8,0},{16,24},{24,16},{32,40},{40,32},{48,56},{56,48},{64,72... | collective-permute-start | bytes 712712 | tf_op jit(solution)/shard_map/ppermute | solution.py:27
  14.3 13.4 %collective-permute-start.3 = (f32[464,128]{1,0:T(8,128)S(1)}, f32[464,128]{1,0:T(8,128)S(1)}, u32[]{:S(2)}, u32[]{:S(2)}) collective-permute-start(f32[464,128]{1,0:T(8,128)S(1)} %get-tuple-element.43), channel_id=1, source_target_pairs={{8,16},{16,8},{24,32},{32,24},{40,48},{48,40},{56,64},{64,56},{72,... | collective-permute-start | bytes 712712 | tf_op jit(solution)/shard_map/ppermute | solution.py:27

commit v4 on v3

--- a/solution.py
+++ b/solution.py
@@ -177,16 +177,27 @@
     return copies
 
 
+LATE = (8, NY - 16)
+
+
+def load_pairs(at, n, arrays, refs, first, count):
+    e, h, p, mat, via, fill = arrays
+    ex, hx, px, cx, fx = refs
+    planes, there = pl.ds(first, count), pl.ds(at, n)
+    dst, here = pl.ds(LOW + first, count), pl.ds(R0 + at, n)
+    pairs = [(a.at[:, planes, there], b.at[:, dst, here]) for a, b in ((e, ex), (h, hx), (p, px))]
+    return pairs + [(a.at[planes, there], b.at[k, dst, here]) for a, b, k in ((mat, cx, 0), (via, cx, 1), (fill, fx, 0))]
+
+
 def load_and_pack(e, h, p, mat, via, fill, perm, cond, stre, rlx, conf, ex, hx, px, cx, fx, tab, out_c, out_d, out_a, out_b, *scratch):
     smalls, sems = scratch[:5], scratch[5]
-    own = pl.ds(LOW, NX)
     copies = []
-    for at, n in ((0, 8), (NY - 8, 8), (8, NY - 16)):
-        there, here = pl.ds(at, n), pl.ds(R0 + at, n)
-        pairs = [(a.at[:, :, there], b.at[:, own, here]) for a, b in ((e, ex), (h, hx), (p, px))]
-        pairs += [(a.at[:, there], b.at[k, own, here]) for a, b, k in ((mat, cx, 0), (via, cx, 1), (fill, fx, 0))]
-        copies += copy_all(pairs, sems.at[pl.ds(len(copies), 6)])
-    few = copy_all(zip((perm, cond, stre, rlx, conf), smalls), sems.at[pl.ds(18, 5)])
+    refs = (e, h, p, mat, via, fill), (ex, hx, px, cx, fx)
+    for at in (0, NY - 8):
+        copies += copy_all(load_pairs(at, 8, *refs, 0, NX), sems.at[pl.ds(len(copies), 6)])
+    for first in (0, NX - 2):
+        copies += copy_all(load_pairs(*LATE, *refs, first, 2), sems.at[pl.ds(len(copies), 6)])
+    few = copy_all(zip((perm, cond, stre, rlx, conf), smalls), sems.at[pl.ds(24, 5)])
     for copy in few:
         copy.wait()
     make_tables(*smalls, tab)
@@ -252,14 +263,18 @@
         slab(out_a, LOW, LOW + 1)
 
 
-def own_coefs(cx, fx, tab, w):
+def near_coefs(e, h, p, mat, via, fill, tab, *refs):
+    ex, hx, px, cx, fx, w, sems = refs[5:]
+    arrays, ext = (e, h, p, mat, via, fill), (ex, hx, px, cx, fx)
+    copies = copy_all(load_pairs(*LATE, arrays, ext, 2, 2), sems.at[pl.ds(0, 6)])
+    copies += copy_all(load_pairs(*LATE, arrays, ext, NX - 4, 2), sems.at[pl.ds(6, 6)])
     b = Block(None, None, None, cx, fx, w)
-
-    def body(x, _):
-        b.coef(x, tab, OWN)
-        return 0
-
-    lax.fori_loop(0, NX, body, 0, unroll=2)
+    b.coef(1, tab, OWN)
+    b.coef(NX - 2, tab, OWN)
+    for copy in copies:
+        copy.wait()
+    b.coef(2, tab, OWN)
+    b.coef(NX - 3, tab, OWN)
 
 
 def first_edges(row_c, row_d, tab, *refs):
@@ -337,12 +352,19 @@
         message(out_a, False)
 
 
-def interior(cx, fx, tab, *refs):
-    ex, hx, px, w = refs[4:]
+def interior(e, h, p, mat, via, fill, tab, *refs):
+    ex, hx, px, cx, fx, w, sems = refs[6:]
+    copies = copy_all(load_pairs(*LATE, (e, h, p, mat, via, fill), (ex, hx, px, cx, fx), 4, NX - 8), sems)
     b = Block(ex, hx, px, cx, fx, w)
     b.masks()
-    for x in (0, *range(3, NX - 3), NX - 1):
+    for x in (0, 3, NX - 4, NX - 1):
+        b.coef(x, tab, range(TILES))
+    for x in range(4, NX - 4):
         b.coef(x, tab, HALO)
+    for copy in copies:
+        copy.wait()
+    for x in range(4, NX - 4):
+        b.coef(x, tab, OWN)
     b.sweep((3, NX - 5), (3, NX - 4))
     b.sweep((2, NX - 4), (2, NX - 3))
     b.sweep((2, NX - 4), (3, NX - 4))
@@ -361,10 +383,53 @@
         b.coef(x, tab, OWN)
 
 
-def last_edges(got2_a, got2_b, tab, *refs):
+def edge(which, got2, tab, b):
+    b.masks()
+    n = RE - R0
+    above = lax.axis_index("gx") % 2 == which
+
+    def take(below):
+        at = MSG2 * n
+        b.take_tiles(below, lambda k: got2[at + 8 * k:at + 8 * k + 8], slice(RH, RE))
+        d1, d2, d3 = (LOW - 1, LOW - 2, LOW - 3) if below else (LOW + NX, LOW + NX + 1, None)
+        if below:
+            planes = [(b.h, c, d2) for c in range(3)] + [(b.e, c, d2) for c in range(3)] + [(b.h, c, d3) for c in (1, 2)]
+        else:
+            planes = [(b.h, c, d1) for c in range(3)] + [(b.h, c, d2) for c in range(3)] + [(b.e, c, d2) for c in (1, 2)]
+        for k, (ref, c, i) in enumerate(planes):
+            ref[c, i, R0:RE] = got2[n * k:n * k + n]
+        for i in (d1, d2):
+            for c in (0, 2):
+                b.e[c, i, RE:RE + 1] = b.e[c, i, R0:R0 + 1]
+                b.h[c, i, R0 - 1:R0] = b.h[c, i, RE - 1:RE]
+
+    @pl.when(above)
+    def _():
+        take(False)
+        for x in (NX, NX + 1):
+            b.coef(x, tab, HALO)
+        b.sweep((NX - 1, NX - 1), (NX - 1, NX))
+        b.sweep((NX - 2, NX), (NX - 2, NX + 1))
+        b.sweep((NX - 3, NX), (NX - 3, NX))
+        b.sweep((NX - 4, NX - 1), (NX - 4, NX - 1), OWN)
+
+    @pl.when(jnp.logical_not(above))
+    def _():
+        take(True)
+        for x in (-2, -1):
+            b.coef(x, tab, HALO)
+        b.sweep((-1, -1), (-1, 0))
+        b.sweep((-2, 0), (-2, 1))
+        b.sweep((-2, 1), (-1, 2))
+        b.sweep((-1, 2), (0, 3), OWN)
+
+
+def edge_a(got2, tab, *refs):
+    edge(0, got2, tab, Block(*refs[6:]))
+
+
+def edge_b(got2, tab, *refs):
     e_out, h_out, p_out, ex, hx, px, cx, fx, w, sems = refs[6:]
-    b = Block(ex, hx, px, cx, fx, w)
-    b.masks()
     rows = pl.ds(R0, NY)
     done = []
 
@@ -374,37 +439,10 @@
             pairs.append((src.at[:, pl.ds(LOW + first, count), rows], dst.at[:, pl.ds(first, count)]))
         done.extend(copy_all(pairs, sems.at[pl.ds(len(done), 3)]))
 
-    store(4, NX - 8)
-    n = RE - R0
-
-    def take(m2, below):
-        at = MSG2 * n
-        b.take_tiles(below, lambda k: m2[at + 8 * k:at + 8 * k + 8], slice(RH, RE))
-        d1, d2, d3 = (LOW - 1, LOW - 2, LOW - 3) if below else (LOW + NX, LOW + NX + 1, None)
-        if below:
-            planes = [(hx, c, d2) for c in range(3)] + [(ex, c, d2) for c in range(3)] + [(hx, c, d3) for c in (1, 2)]
-        else:
-            planes = [(hx, c, d1) for c in range(3)] + [(hx, c, d2) for c in range(3)] + [(ex, c, d2) for c in (1, 2)]
-        for k, (ref, c, i) in enumerate(planes):
-            ref[c, i, R0:RE] = m2[n * k:n * k + n]
-        for i in (d1, d2):
-            for c in (0, 2):
-                ex[c, i, RE:RE + 1] = ex[c, i, R0:R0 + 1]
-                hx[c, i, R0 - 1:R0] = hx[c, i, RE - 1:RE]
-
-    for_sides(take, (got2_a,), (got2_b,))
-    for x in (-2, -1, NX, NX + 1):
-        b.coef(x, tab, HALO)
-    b.sweep((-1, -1), (-1, 0))
-    b.sweep((-2, 0), (-2, 1))
-    b.sweep((-2, 1), (-1, 2))
-    b.sweep((-1, 2), (0, 3), OWN)
-    store(0, 4)
-    b.sweep((NX - 1, NX - 1), (NX - 1, NX))
-    b.sweep((NX - 2, NX), (NX - 2, NX + 1))
-    b.sweep((NX - 3, NX), (NX - 3, NX))
-    b.sweep((NX - 4, NX - 1), (NX - 4, NX - 1), OWN)
-    store(NX - 4, 4)
+    above = lax.axis_index("gx") % 2 == 1
+    store(jnp.where(above, 0, 4), NX - 4)
+    edge(1, got2, tab, Block(ex, hx, px, cx, fx, w))
+    store(jnp.where(above, NX - 4, 0), 4)
     for copy in done:
         copy.wait()
 
@@ -427,17 +465,19 @@
     ex, hx, px, cx, fx, tab, strip_c, strip_d, slab_a, slab_b = pl.pallas_call(
         load_and_pack, out_shape=(field, field, field, ints, fill, shape((18, 8, NZ), F32), strip, strip, slab1, slab1),
         in_specs=[hbm] * 11, out_specs=(vmem,) * 10,
-        scratch_shapes=[pltpu.SMEM((3,), F32)] * 4 + [pltpu.SMEM((3, 8), F32), pltpu.SemaphoreType.DMA((23,))],
+        scratch_shapes=[pltpu.SMEM((3,), F32)] * 4 + [pltpu.SMEM((3, 8), F32), pltpu.SemaphoreType.DMA((29,))],
         compiler_params=params, name="load_and_pack",
     )(*cells, *tables)
     row_c = swapped(strip_c, "gy", 0)
     row_d = swapped(strip_d, "gy", 1)
     got1_a = swapped(slab_a, "gx", 0)
     got1_b = swapped(slab_b, "gx", 1)
-    w = pl.pallas_call(
-        own_coefs, out_shape=coef, in_specs=[vmem] * 3, out_specs=vmem, compiler_params=params, name="own_coefs",
+    ex, hx, px, cx, fx, w = pl.pallas_call(
+        near_coefs, out_shape=(field, field, field, ints, fill, coef), in_specs=[hbm] * 6 + [vmem] * 6, out_specs=(vmem,) * 6,
+        input_output_aliases={7 + k: k for k in range(5)}, scratch_shapes=[pltpu.SemaphoreType.DMA((12,))],
+        compiler_params=params, name="near_coefs",
         cost_estimate=pl.CostEstimate(flops=10_000_000, bytes_accessed=4_000_000, transcendentals=0),
-    )(cx, fx, tab)
+    )(*cells, tab, ex, hx, px, cx, fx)
     ex, hx, px, cx, fx, w, send_a, send_b = pl.pallas_call(
         first_edges, out_shape=(field, field, field, ints, fill, coef, slab2, slab2),
         in_specs=[vmem] * 9, out_specs=(vmem,) * 8,
@@ -445,23 +485,27 @@
     )(row_c, row_d, tab, ex, hx, px, cx, fx, w)
     got2_a = swapped(send_a, "gx", 0)
     got2_b = swapped(send_b, "gx", 1)
-    ex, hx, px, w = pl.pallas_call(
-        interior, out_shape=(field, field, field, coef),
-        in_specs=[vmem] * 7, out_specs=(vmem,) * 4,
-        input_output_aliases={3 + k: k for k in range(4)}, compiler_params=params, name="interior",
-        cost_estimate=pl.CostEstimate(flops=80_000_000, bytes_accessed=20_000_000, transcendentals=0),
-    )(cx, fx, tab, ex, hx, px, w)
     state = (ex, hx, px, cx, fx, w)
     shapes = (field, field, field, ints, fill, coef)
+    state = pl.pallas_call(
+        interior, out_shape=shapes, in_specs=[hbm] * 6 + [vmem] * 7, out_specs=(vmem,) * 6,
+        input_output_aliases={7 + k: k for k in range(6)}, scratch_shapes=[pltpu.SemaphoreType.DMA((6,))],
+        compiler_params=params, name="interior",
+        cost_estimate=pl.CostEstimate(flops=80_000_000, bytes_accessed=20_000_000, transcendentals=0),
+    )(*cells, tab, *state)
     state = pl.pallas_call(
         neighbour_cells, out_shape=shapes, in_specs=[vmem] * 9, out_specs=(vmem,) * 6,
         input_output_aliases={3 + k: k for k in range(6)}, compiler_params=params, name="neighbour_cells",
     )(got1_a, got1_b, tab, *state)
+    state = pl.pallas_call(
+        edge_a, out_shape=shapes, in_specs=[vmem] * 8, out_specs=(vmem,) * 6,
+        input_output_aliases={2 + k: k for k in range(6)}, compiler_params=params, name="edge_a",
+    )(got2_a, tab, *state)
     outs = pl.pallas_call(
-        last_edges, out_shape=(result,) * 3 + shapes, in_specs=[vmem] * 9, out_specs=(hbm,) * 3 + (vmem,) * 6,
-        input_output_aliases={3 + k: 3 + k for k in range(6)},
-        scratch_shapes=[pltpu.SemaphoreType.DMA((9,))], compiler_params=params, name="last_edges",
-    )(got2_a, got2_b, tab, *state)
+        edge_b, out_shape=(result,) * 3 + shapes, in_specs=[vmem] * 8, out_specs=(hbm,) * 3 + (vmem,) * 6,
+        input_output_aliases={2 + k: 3 + k for k in range(6)},
+        scratch_shapes=[pltpu.SemaphoreType.DMA((6,))], compiler_params=params, name="edge_b",
+    )(got2_b, tab, *state)
     return outs[:3]
 
 

time: 30.6 us -> 29.4 us (0.961)
  waiting for transfers between devices: 6.18 us -> 3.2 us
  Pallas kernels: 10.3 us -> 11.6 us
    ppermute x6, waiting for transfers between devices: 6.18 us -> 3.2 us  [swapped(): return lax.ppermute(value, axis, pairs)]
    pallas_call x3 -> x4, Pallas kernels: 7.25 us -> 8.94 us  [the longest x1 4.95 us: shards(): pl.pallas_call(interior, out_shape=shapes, in_specs=[hbm] * 6 + [vmem] *...]
    pallas_call x1, Pallas kernels: 2.24 us -> 1.89 us  [shards(): pl.pallas_call(load_and_pack, out_shape=(field, field, field, ints, fill,...]
  transfers between devices with their start and end apart: 6 -> 6, of which waited for: 3 -> 1; matrix products, arithmetic and copies ran while one was open for 0% -> 0% of each run, Pallas kernels for 17% -> 27%
where the time goes in v4:
time: 29.4 us; the launch traced here: 29.1 us
  starting transfers between devices  13.5 us (46%)
  Pallas kernels  11.6 us (39%)
  waiting for transfers between devices  3.2 us (11%)
  between operations  0.74 us (3%)
    ppermute x6, starting transfers between devices, swapped(): return lax.ppermute(value, axis, pairs)  13.5 us
    pallas_call x1, Pallas kernels, shards(): pl.pallas_call(interior, out_shape=shapes, in_specs=[hbm] * 6 + [vmem] *...  4.95 us
    ppermute x6, waiting for transfers between devices, swapped(): return lax.ppermute(value, axis, pairs)  3.2 us
    pallas_call x1, Pallas kernels, shards(): pl.pallas_call(load_and_pack, out_shape=(field, field, field, ints, fill,...  1.89 us
    pallas_call x1, Pallas kernels, shards(): pl.pallas_call(edge_b, out_shape=(result,) * 3 + shapes, in_specs=[vmem]...  1.73 us
    pallas_call x1, Pallas kernels, shards(): pl.pallas_call(near_coefs, out_shape=(field, field, field, ints, fill, co...  1.22 us
    pallas_call x1, Pallas kernels, shards(): pl.pallas_call(edge_a, out_shape=shapes, in_specs=[vmem] * 8, out_specs=(...  1.04 us
  transfers between devices with their start and end apart: 6, of which 1 were waited for; matrix products, arithmetic and copies ran while one was open for 0% of the time, Pallas kernels for 27%

profile of v4, /device:TPU:130, one launch (start us, length us, event | category | flops | bytes accessed | tf_op | source)
XLA Modules:
  0.0 29.1 jit_solution(17156233778599204625)
XLA Ops:
  0.6 1.9 %load_and_pack.1 = (f32[3,21,56,128]{3,2,1,0:T(8,128)S(1)}, f32[3,21,56,128]{3,2,1,0:T(8,128)S(1)}, f32[3,21,56,128]{3,2,1,0:T(8,128)S(1)}, s32[2,21,56,128]{3,2...) custom-call(f32[3,16,32,128]{3,2,1,0:T(8,128)} %e.5, ...), custom_call_target="tpu_custom_call" | custom-call | tf_op jit(solution)/shard_map/load_and_pack/pallas_call | solution.py:465
  2.5 0.1 collective-permute-start
  2.6 2.5 %collective-permute-start.1 = (f32[6,16,8,128]{3,2,1,0:T(8,128)S(1)}, f32[6,16,8,128]{3,2,1,0:T(8,128)S(1)}, u32[]{:S(2)}, u32[]{:S(2)}) collective-permute-start(f32[6,16,8,128]{3,2,1,0:T(8,128)S(1)} %get-tuple-element.49), channel_id=1, source_target_pairs={{1,2},{2,1},{3,4},{4,3},{5,6},{6,5},{9,10},{10,9},{11,12},{12,11},... | collective-permute-start | bytes 1179656 | tf_op jit(solution)/shard_map/ppermute | solution.py:27
  5.2 1.7 %collective-permute-start.4 = (f32[18,32,128]{2,1,0:T(8,128)S(1)}, f32[18,32,128]{2,1,0:T(8,128)S(1)}, u32[]{:S(2)}, u32[]{:S(2)}) collective-permute-start(f32[18,32,128]{2,1,0:T(8,128)S(1)} %get-tuple-element.64), channel_id=1, source_target_pairs={{0,8},{8,0},{16,24},{24,16},{32,40},{40,32},{48,56},{56,48},{64,72... | collective-permute-start | bytes 884744 | tf_op jit(solution)/shard_map/ppermute | solution.py:27
  6.8 3.6 %collective-permute-start.5 = (f32[18,32,128]{2,1,0:T(8,128)S(1)}, f32[18,32,128]{2,1,0:T(8,128)S(1)}, u32[]{:S(2)}, u32[]{:S(2)}) collective-permute-start(f32[18,32,128]{2,1,0:T(8,128)S(1)} %get-tuple-element.65), channel_id=1, source_target_pairs={{8,16},{16,8},{24,32},{32,24},{40,48},{48,40},{56,64},{64,56},{72,... | collective-permute-start | bytes 884744 | tf_op jit(solution)/shard_map/ppermute | solution.py:27
  10.5 1.2 %near_coefs.1 = (f32[3,21,56,128]{3,2,1,0:T(8,128)S(1)}, f32[3,21,56,128]{3,2,1,0:T(8,128)S(1)}, f32[3,21,56,128]{3,2,1,0:T(8,128)S(1)}, s32[2,21,56,128]{3,2,1,...) custom-call(f32[3,16,32,128]{3,2,1,0:T(8,128)} %e.5, ...), custom_call_target="tpu_custom_call", output_to_operand_aliasing={{0}: (7, {}), {1}: (8, {}), {2}: (9, {}), {3}: (10, {}), {4... | custom-call | flops 10000000 | bytes 4000000 | tf_op jit(solution)/shard_map/near_coefs/pallas_call | solution.py:475
  11.7 0.0 collective-permute-done.row_c
  11.7 0.0 collective-permute-done.1.row_d
  11.7 0.6 %first_edges.1 = (f32[3,21,56,128]{3,2,1,0:T(8,128)S(1)}, f32[3,21,56,128]{3,2,1,0:T(8,128)S(1)}, f32[3,21,56,128]{3,2,1,0:T(8,128)S(1)}, s32[2,21,56,128]{3,2,1...) custom-call(f32[6,16,8,128]{3,2,1,0:T(8,128)S(1)} %collective-permut, ...), custom_call_target="tpu_custom_call", output_to_operand_aliasing={{0}: (3, {}), {1}: (4, {}), {2}: (5, {}), {3}: (6, {}), {4}... | custom-call | tf_op jit(solution)/shard_map/first_edges/pallas_call | solution.py:481
  12.3 1.7 %collective-permute-start.3 = (f32[464,128]{1,0:T(8,128)S(1)}, f32[464,128]{1,0:T(8,128)S(1)}, u32[]{:S(2)}, u32[]{:S(2)}) collective-permute-start(f32[464,128]{1,0:T(8,128)S(1)} %get-tuple-element.63), channel_id=1, source_target_pairs={{0,8},{8,0},{16,24},{24,16},{32,40},{40,32},{48,56},{56,48},{64,72... | collective-permute-start | bytes 712712 | tf_op jit(solution)/shard_map/ppermute | solution.py:27
  14.0 4.0 %collective-permute-start.2 = (f32[464,128]{1,0:T(8,128)S(1)}, f32[464,128]{1,0:T(8,128)S(1)}, u32[]{:S(2)}, u32[]{:S(2)}) collective-permute-start(f32[464,128]{1,0:T(8,128)S(1)} %get-tuple-element.62), channel_id=1, source_target_pairs={{8,16},{16,8},{24,32},{32,24},{40,48},{48,40},{56,64},{64,56},{72,... | collective-permute-start | bytes 712712 | tf_op jit(solution)/shard_map/ppermute | solution.py:27
  18.0 5.0 %interior.1 = (f32[3,21,56,128]{3,2,1,0:T(8,128)S(1)}, f32[3,21,56,128]{3,2,1,0:T(8,128)S(1)}, f32[3,21,56,128]{3,2,1,0:T(8,128)S(1)}, s32[2,21,56,128]{3,2,1,0:...) custom-call(f32[3,16,32,128]{3,2,1,0:T(8,128)} %e.5, ...), custom_call_target="tpu_custom_call", output_to_operand_aliasing={{0}: (7, {}), {1}: (8, {}), {2}: (9, {}), {3}: (10, {}), {4... | custom-call | flops 80000000 | bytes 20000000 | tf_op jit(solution)/shard_map/interior/pallas_call | solution.py:490
  22.9 0.0 collective-permute-done.4.got1_a
  22.9 0.0 collective-permute-done.5.got1_b
  22.9 0.2 neighbour_cells.1
  23.2 0.0 collective-permute-done.3.got2
  23.2 1.0 %edge_a.1 = (f32[3,21,56,128]{3,2,1,0:T(8,128)S(1)}, f32[3,21,56,128]{3,2,1,0:T(8,128)S(1)}, f32[3,21,56,128]{3,2,1,0:T(8,128)S(1)}, s32[2,21,56,128]{3,2,1,0:T(...) custom-call(f32[464,128]{1,0:T(8,128)S(1)} %collective-permute-done., ...), custom_call_target="tpu_custom_call", output_to_operand_aliasing={{0}: (2, {}), {1}: (3, {}), {2}: (4, {}), {3}: (5, {}), {4}... | custom-call | tf_op jit(solution)/shard_map/edge_a/pallas_call | solution.py:500
  24.2 3.2 %collective-permute-done.2.got2 = f32[464,128]{1,0:T(8,128)S(1)} collective-permute-done((f32[464,128]{1,0:T(8,128)S(1)}, f32[464,128]{1,0:T(8,128)S(1)}, u32[]{:S(2)}, u32[]{:S(2)}) %collective-permute-start.2) | collective-permute-done | bytes 237600 | tf_op jit(solution)/shard_map/ppermute | solution.py:27
  27.4 1.7 %edge_b.1 = (f32[3,16,32,128]{3,2,1,0:T(8,128)}, f32[3,16,32,128]{3,2,1,0:T(8,128)}, f32[3,16,32,128]{3,2,1,0:T(8,128)}, f32[3,21,56,128]{3,2,1,0:T(8,128)S(1)},...) custom-call(f32[464,128]{1,0:T(8,128)S(1)} %collective-permute-done., ...), custom_call_target="tpu_custom_call", output_to_operand_aliasing={{3}: (2, {}), {4}: (3, {}), {5}: (4, {}), {6}: (5, {}), {7}... | custom-call | tf_op jit(solution)/shard_map/edge_b/pallas_call | solution.py:504
Async XLA Ops:
  2.5 9.2 %collective-permute-start = (f32[6,16,8,128]{3,2,1,0:T(8,128)S(1)}, f32[6,16,8,128]{3,2,1,0:T(8,128)S(1)}, u32[]{:S(2)}, u32[]{:S(2)}) collective-permute-start(f32[6,16,8,128]{3,2,1,0:T(8,128)S(1)} %get-tuple-element.48), channel_id=1, source_target_pairs={{0,1},{1,0},{2,3},{3,2},{4,5},{5,4},{6,7},{7,6},{8,9},{9,8},{10,11... | collective-permute-start | bytes 1179656 | tf_op jit(solution)/shard_map/ppermute | solution.py:27
  2.6 9.1 %collective-permute-start.1 = (f32[6,16,8,128]{3,2,1,0:T(8,128)S(1)}, f32[6,16,8,128]{3,2,1,0:T(8,128)S(1)}, u32[]{:S(2)}, u32[]{:S(2)}) collective-permute-start(f32[6,16,8,128]{3,2,1,0:T(8,128)S(1)} %get-tuple-element.49), channel_id=1, source_target_pairs={{1,2},{2,1},{3,4},{4,3},{5,6},{6,5},{9,10},{10,9},{11,12},{12,11},... | collective-permute-start | bytes 1179656 | tf_op jit(solution)/shard_map/ppermute | solution.py:27
  5.2 17.7 %collective-permute-start.4 = (f32[18,32,128]{2,1,0:T(8,128)S(1)}, f32[18,32,128]{2,1,0:T(8,128)S(1)}, u32[]{:S(2)}, u32[]{:S(2)}) collective-permute-start(f32[18,32,128]{2,1,0:T(8,128)S(1)} %get-tuple-element.64), channel_id=1, source_target_pairs={{0,8},{8,0},{16,24},{24,16},{32,40},{40,32},{48,56},{56,48},{64,72... | collective-permute-start | bytes 884744 | tf_op jit(solution)/shard_map/ppermute | solution.py:27
  6.8 16.1 %collective-permute-start.5 = (f32[18,32,128]{2,1,0:T(8,128)S(1)}, f32[18,32,128]{2,1,0:T(8,128)S(1)}, u32[]{:S(2)}, u32[]{:S(2)}) collective-permute-start(f32[18,32,128]{2,1,0:T(8,128)S(1)} %get-tuple-element.65), channel_id=1, source_target_pairs={{8,16},{16,8},{24,32},{32,24},{40,48},{48,40},{56,64},{64,56},{72,... | collective-permute-start | bytes 884744 | tf_op jit(solution)/shard_map/ppermute | solution.py:27
  12.3 10.9 %collective-permute-start.3 = (f32[464,128]{1,0:T(8,128)S(1)}, f32[464,128]{1,0:T(8,128)S(1)}, u32[]{:S(2)}, u32[]{:S(2)}) collective-permute-start(f32[464,128]{1,0:T(8,128)S(1)} %get-tuple-element.63), channel_id=1, source_target_pairs={{0,8},{8,0},{16,24},{24,16},{32,40},{40,32},{48,56},{56,48},{64,72... | collective-permute-start | bytes 712712 | tf_op jit(solution)/shard_map/ppermute | solution.py:27
  14.0 13.4 %collective-permute-start.2 = (f32[464,128]{1,0:T(8,128)S(1)}, f32[464,128]{1,0:T(8,128)S(1)}, u32[]{:S(2)}, u32[]{:S(2)}) collective-permute-start(f32[464,128]{1,0:T(8,128)S(1)} %get-tuple-element.62), channel_id=1, source_target_pairs={{8,16},{16,8},{24,32},{32,24},{40,48},{48,40},{56,64},{64,56},{72,... | collective-permute-start | bytes 712712 | tf_op jit(solution)/shard_map/ppermute | solution.py:27

commit v5 on v4

--- a/solution.py
+++ b/solution.py
@@ -14,7 +14,7 @@
 EXT = (NX + LOW + HIGH, RE + 8, NZ)
 TILES = (RE - R0) // 8
 OWN, HALO = range(TILES - 1), range(TILES - 1, TILES)
-MSG1, MSG2 = 18, 8
+MSG1, MSG2 = 15, 7
 MSG2_ROWS = MSG2 * (RE - R0) + MSG1 * 8
 
 ORDER = (("e", 0), ("e", 1), ("e", 2), ("h", 0), ("h", 1), ("h", 2), ("p", 0), ("p", 1), ("p", 2), ("f", 0), ("c", 0), ("c", 1))
@@ -101,13 +101,12 @@
         for c in range(3):
             self.e[c, d1, rows] = part(c)
             self.p[c, d1, rows] = part(3 + c)
-            self.p[c, d2, rows] = part(12 + c)
+            self.w[4 + c, d2, rows] = part(9 + c)
             if below:
-                self.h[c, d1, rows] = part(15 + c)
-        for k, i in ((6, d1), (9, d2)):
-            self.c[0, i, rows] = part(k).astype(jnp.int32)
-            self.c[1, i, rows] = part(k + 1).astype(jnp.int32)
-            self.f[0, i, rows] = part(k + 2)
+                self.h[c, d1, rows] = part(12 + c)
+        self.c[0, d1, rows] = part(6).astype(jnp.int32)
+        self.c[1, d1, rows] = part(7).astype(jnp.int32)
+        self.f[0, d1, rows] = part(8)
 
     def h_plane(self, x):
         i = x + LOW
@@ -155,6 +154,82 @@
             if e_planes[0] <= x <= e_planes[1]:
                 self.e_plane(x, tiles)
 
+    def mask(self, x, t):
+        inside = self.plane_in(x)
+        m = DT if inside is None else DT * inside
+        return self.row_in * m if t == TILES - 1 else m
+
+    def below_second(self):
+        i = LOW - 2
+        e, h, p, w = self.e, self.h, self.p, self.w
+        for t in range(TILES):
+            r = slice(R0 + 8 * t, R0 + 8 * t + 8)
+            m = self.mask(-2, t)
+            h[1, i, r] = e[1, i, r] + m * e[2, i + 1, r]
+            h2 = e[2, i, r] - m * e[1, i + 1, r]
+            h[2, i, r] = h2
+        h[2, i, R0 - 1:R0] = h2[7:8]
+        for t in range(TILES):
+            a = R0 + 8 * t
+            r, down = slice(a, a + 8), slice(a - 1, a + 7)
+            h1, h2 = h[1, i, r], h[2, i, r]
+            e0 = p[0, i, r] + w[4, i, r] * ((h2 - h[2, i, down]) - (h1 - self.zb(h1)))
+            e2 = p[2, i, r] + w[6, i, r] * h1
+            e[0, i, r], e[1, i, r], e[2, i, r] = e0, p[1, i, r] - w[5, i, r] * h2, e2
+            if t == 0:
+                e[0, i, RE:RE + 1] = e0[0:1]
+                e[2, i, RE:RE + 1] = e2[0:1]
+
+    def above_second(self):
+        i = LOW + NX + 1
+        for t in range(TILES):
+            r = slice(R0 + 8 * t, R0 + 8 * t + 8)
+            self.e[1, i, r] = self.p[1, i, r] + self.w[5, i, r] * self.h[2, i - 1, r]
+            self.e[2, i, r] = self.p[2, i, r] - self.w[6, i, r] * self.h[1, i - 1, r]
+
+    def for_above(self, out, tmp):
+        i, n = LOW + NX - 2, RE - R0
+        e, h, p, w = self.e, self.h, self.p, self.w
+        for t in range(TILES):
+            a, o = R0 + 8 * t, 8 * t
+            r, up = slice(a, a + 8), slice(a + 1, a + 9)
+            e0, e1, e2 = e[0, i, r], e[1, i, r], e[2, i, r]
+            h1, h2 = h[1, i, r], h[2, i, r]
+            m = self.mask(NX - 2, t)
+            h0 = h[0, i, r] - m * ((e[2, i, up] - e2) - (self.zf(e1) - e1))
+            tmp[r] = h0
+            out[o:o + 8] = h1
+            out[n + o:n + o + 8] = h2
+            out[2 * n + o:2 * n + o + 8] = h1 - m * ((self.zf(e0) - e0) + e2)
+            out[3 * n + o:3 * n + o + 8] = h2 + m * (e1 + (e[0, i, up] - e0))
+        tmp[R0 - 1:R0] = h0[7:8]
+        for t in range(TILES):
+            a, o = R0 + 8 * t, 8 * t
+            r, down = slice(a, a + 8), slice(a - 1, a + 7)
+            h0 = tmp[r]
+            w0, w1 = w[0, i, r], w[1, i, r]
+            part = [w0 * e[c, i, r] + w1 * p[c, i, r] for c in range(3)]
+            part[1] += w[5, i, r] * ((h0 - self.zb(h0)) + h[2, i - 1, r])
+            part[2] -= w[6, i, r] * (h[1, i - 1, r] + (h0 - tmp[down]))
+            for c in range(3):
+                at = (4 + c) * n + o
+                out[at:at + 8] = part[c]
+
+    def for_below(self, out):
+        i, n = LOW + 1, RE - R0
+        e, h, p, w = self.e, self.h, self.p, self.w
+        for k, (ref, c, at) in enumerate([(h, c, LOW) for c in range(3)] + [(e, 1, i), (e, 2, i)]):
+            out[n * k:n * k + n] = ref[c, at, R0:RE]
+        for t in range(TILES):
+            a, o = R0 + 8 * t, 8 * t
+            r, down = slice(a, a + 8), slice(a - 1, a + 7)
+            h0, h1, h2 = h[0, i, r], h[1, i, r], h[2, i, r]
+            w0, w1 = w[0, i, r], w[1, i, r]
+            part1 = w0 * e[1, i, r] + w1 * p[1, i, r] + w[5, i, r] * ((h0 - self.zb(h0)) - h2)
+            part2 = w0 * e[2, i, r] + w1 * p[2, i, r] + w[6, i, r] * (h1 - (h0 - h[0, i, down]))
+            out[5 * n + o:5 * n + o + 8] = part1
+            out[6 * n + o:6 * n + o + 8] = part2
+
 
 def for_sides(take, from_a, from_b):
     odd = lax.axis_index("gx") % 2
@@ -189,14 +264,14 @@
     return pairs + [(a.at[planes, there], b.at[k, dst, here]) for a, b, k in ((mat, cx, 0), (via, cx, 1), (fill, fx, 0))]
 
 
-def load_and_pack(e, h, p, mat, via, fill, perm, cond, stre, rlx, conf, ex, hx, px, cx, fx, tab, out_c, out_d, out_a, out_b, *scratch):
+def load_and_pack(e, h, p, mat, via, fill, perm, cond, stre, rlx, conf, ex, hx, px, cx, fx, tab, w, out_c, out_d, out_a, out_b, *scratch):
     smalls, sems = scratch[:5], scratch[5]
     copies = []
     refs = (e, h, p, mat, via, fill), (ex, hx, px, cx, fx)
     for at in (0, NY - 8):
         copies += copy_all(load_pairs(at, 8, *refs, 0, NX), sems.at[pl.ds(len(copies), 6)])
-    for first in (0, NX - 2):
-        copies += copy_all(load_pairs(*LATE, *refs, first, 2), sems.at[pl.ds(len(copies), 6)])
+    for first in (0, NX - 4):
+        copies += copy_all(load_pairs(*LATE, *refs, first, 4), sems.at[pl.ds(len(copies), 6)])
     few = copy_all(zip((perm, cond, stre, rlx, conf), smalls), sems.at[pl.ds(24, 5)])
     for copy in few:
         copy.wait()
@@ -236,21 +311,19 @@
         copy.wait()
     own_rows = slice(R0, RH)
 
+    b = Block(ex, hx, px, cx, fx, w)
+    for x in (1, NX - 2):
+        b.coef(x, tab, OWN)
+
     def slab(out, d1, d2):
         for c in range(3):
             out[c] = ex[c, d1, own_rows]
             out[3 + c] = px[c, d1, own_rows]
-            out[15 + c] = hx[c, d1, own_rows]
-        for k, i in ((6, d1), (9, d2)):
-            out[k] = cx[0, i, own_rows].astype(F32)
-            out[k + 1] = cx[1, i, own_rows].astype(F32)
-            out[k + 2] = fx[0, i, own_rows]
-        for t in range(NY // 8):
-            r = slice(R0 + 8 * t, R0 + 8 * t + 8)
-            m = cx[0, d2, r]
-            kp, bp = pick(tab, m, 2), pick(tab, m, 3)
-            for c in range(3):
-                out[12 + c, 8 * t:8 * t + 8] = kp * px[c, d2, r] + bp * ex[c, d2, r]
+            out[9 + c] = w[4 + c, d2, own_rows]
+            out[12 + c] = hx[c, d1, own_rows]
+        out[6] = cx[0, d1, own_rows].astype(F32)
+        out[7] = cx[1, d1, own_rows].astype(F32)
+        out[8] = fx[0, d1, own_rows]
 
     @pl.when(gx_odd == 0)
     def _():
@@ -263,22 +336,8 @@
         slab(out_a, LOW, LOW + 1)
 
 
-def near_coefs(e, h, p, mat, via, fill, tab, *refs):
-    ex, hx, px, cx, fx, w, sems = refs[5:]
-    arrays, ext = (e, h, p, mat, via, fill), (ex, hx, px, cx, fx)
-    copies = copy_all(load_pairs(*LATE, arrays, ext, 2, 2), sems.at[pl.ds(0, 6)])
-    copies += copy_all(load_pairs(*LATE, arrays, ext, NX - 4, 2), sems.at[pl.ds(6, 6)])
-    b = Block(None, None, None, cx, fx, w)
-    b.coef(1, tab, OWN)
-    b.coef(NX - 2, tab, OWN)
-    for copy in copies:
-        copy.wait()
-    b.coef(2, tab, OWN)
-    b.coef(NX - 3, tab, OWN)
-
-
 def first_edges(row_c, row_d, tab, *refs):
-    ex, hx, px, cx, fx, w, out_a, out_b = refs[6:]
+    ex, hx, px, cx, fx, w, out_a, out_b, tmp = refs[6:]
     b = Block(ex, hx, px, cx, fx, w)
     b.masks()
     named = {"e": ex, "h": hx, "p": px, "c": cx, "f": fx}
@@ -310,8 +369,10 @@
     def _():
         all_rows(row_d, row_c)
 
-    for x in (1, 2, NX - 3, NX - 2):
+    for x in (1, NX - 2):
         b.coef(x, tab, HALO)
+    for x in (2, NX - 3):
+        b.coef(x, tab, range(TILES))
     b.h_plane(0)
     for x in (1, 2):
         b.h_plane(x)
@@ -326,17 +387,14 @@
     n = RE - R0
 
     def message(out, upward):
-        d1, d2, d3 = (LOW + NX - 1, LOW + NX - 2, LOW + NX - 3) if upward else (LOW, LOW + 1, None)
+        d1, d2 = (LOW + NX - 1, LOW + NX - 2) if upward else (LOW, LOW + 1)
         if upward:
-            planes = [(hx, c, d2) for c in range(3)] + [(ex, c, d2) for c in range(3)] + [(hx, c, d3) for c in (1, 2)]
+            b.for_above(out, tmp)
         else:
-            planes = [(hx, c, d1) for c in range(3)] + [(hx, c, d2) for c in range(3)] + [(ex, c, d2) for c in (1, 2)]
-        for k, (ref, c, i) in enumerate(planes):
-            out[n * k:n * k + n] = ref[c, i, R0:RE]
+            b.for_below(out)
         tiles = [(ex, c, d1) for c in range(3)] + [(px, c, d1) for c in range(3)]
-        for i in (d1, d2):
-            tiles += [(cx, 0, i), (cx, 1, i), (fx, 0, i)]
-        tiles += [(px, c, d2) for c in range(3)] + [(hx, c, d1) for c in range(3)]
+        tiles += [(cx, 0, d1), (cx, 1, d1), (fx, 0, d1)]
+        tiles += [(w, 4 + c, d2) for c in range(3)] + [(hx, c, d1) for c in range(3)]
         for k, (ref, c, i) in enumerate(tiles):
             at = MSG2 * n + 8 * k
             out[at:at + 8] = ref[c, i, RH:RE].astype(F32)
@@ -379,7 +437,7 @@
         b.take_tiles(below, lambda k: m1[k], slice(R0, RH))
 
     for_sides(take, (got1_a,), (got1_b,))
-    for x in (-2, -1, NX, NX + 1):
+    for x in (-1, NX):
         b.coef(x, tab, OWN)
 
 
@@ -391,35 +449,34 @@
     def take(below):
         at = MSG2 * n
         b.take_tiles(below, lambda k: got2[at + 8 * k:at + 8 * k + 8], slice(RH, RE))
-        d1, d2, d3 = (LOW - 1, LOW - 2, LOW - 3) if below else (LOW + NX, LOW + NX + 1, None)
+        d1, d2 = (LOW - 1, LOW - 2) if below else (LOW + NX, LOW + NX + 1)
         if below:
-            planes = [(b.h, c, d2) for c in range(3)] + [(b.e, c, d2) for c in range(3)] + [(b.h, c, d3) for c in (1, 2)]
+            planes = [(b.h, 1, d2), (b.h, 2, d2), (b.e, 1, d2), (b.e, 2, d2)] + [(b.p, c, d2) for c in range(3)]
         else:
-            planes = [(b.h, c, d1) for c in range(3)] + [(b.h, c, d2) for c in range(3)] + [(b.e, c, d2) for c in (1, 2)]
+            planes = [(b.h, c, d1) for c in range(3)] + [(b.e, 1, d2), (b.e, 2, d2), (b.p, 1, d2), (b.p, 2, d2)]
         for k, (ref, c, i) in enumerate(planes):
             ref[c, i, R0:RE] = got2[n * k:n * k + n]
-        for i in (d1, d2):
-            for c in (0, 2):
-                b.e[c, i, RE:RE + 1] = b.e[c, i, R0:R0 + 1]
-                b.h[c, i, R0 - 1:R0] = b.h[c, i, RE - 1:RE]
+        for c in (0, 2):
+            b.e[c, d1, RE:RE + 1] = b.e[c, d1, R0:R0 + 1]
+            b.h[c, d1, R0 - 1:R0] = b.h[c, d1, RE - 1:RE]
 
     @pl.when(above)
     def _():
         take(False)
-        for x in (NX, NX + 1):
-            b.coef(x, tab, HALO)
+        b.coef(NX, tab, HALO)
         b.sweep((NX - 1, NX - 1), (NX - 1, NX))
-        b.sweep((NX - 2, NX), (NX - 2, NX + 1))
+        b.sweep((NX - 2, NX), (NX - 2, NX))
+        b.above_second()
         b.sweep((NX - 3, NX), (NX - 3, NX))
         b.sweep((NX - 4, NX - 1), (NX - 4, NX - 1), OWN)
 
     @pl.when(jnp.logical_not(above))
     def _():
         take(True)
-        for x in (-2, -1):
-            b.coef(x, tab, HALO)
+        b.coef(-1, tab, HALO)
         b.sweep((-1, -1), (-1, 0))
-        b.sweep((-2, 0), (-2, 1))
+        b.below_second()
+        b.sweep((-1, 0), (-1, 1))
         b.sweep((-2, 1), (-1, 2))
         b.sweep((-1, 2), (0, 3), OWN)
 
@@ -462,9 +519,9 @@
     result = shape((3, NX, NY, NZ), F32)
     params = pltpu.CompilerParams(vmem_limit_bytes=4 << 20)
 
-    ex, hx, px, cx, fx, tab, strip_c, strip_d, slab_a, slab_b = pl.pallas_call(
-        load_and_pack, out_shape=(field, field, field, ints, fill, shape((18, 8, NZ), F32), strip, strip, slab1, slab1),
-        in_specs=[hbm] * 11, out_specs=(vmem,) * 10,
+    ex, hx, px, cx, fx, tab, w, strip_c, strip_d, slab_a, slab_b = pl.pallas_call(
+        load_and_pack, out_shape=(field, field, field, ints, fill, shape((18, 8, NZ), F32), coef, strip, strip, slab1, slab1),
+        in_specs=[hbm] * 11, out_specs=(vmem,) * 11,
         scratch_shapes=[pltpu.SMEM((3,), F32)] * 4 + [pltpu.SMEM((3, 8), F32), pltpu.SemaphoreType.DMA((29,))],
         compiler_params=params, name="load_and_pack",
     )(*cells, *tables)
@@ -472,16 +529,11 @@
     row_d = swapped(strip_d, "gy", 1)
     got1_a = swapped(slab_a, "gx", 0)
     got1_b = swapped(slab_b, "gx", 1)
-    ex, hx, px, cx, fx, w = pl.pallas_call(
-        near_coefs, out_shape=(field, field, field, ints, fill, coef), in_specs=[hbm] * 6 + [vmem] * 6, out_specs=(vmem,) * 6,
-        input_output_aliases={7 + k: k for k in range(5)}, scratch_shapes=[pltpu.SemaphoreType.DMA((12,))],
-        compiler_params=params, name="near_coefs",
-        cost_estimate=pl.CostEstimate(flops=10_000_000, bytes_accessed=4_000_000, transcendentals=0),
-    )(*cells, tab, ex, hx, px, cx, fx)
     ex, hx, px, cx, fx, w, send_a, send_b = pl.pallas_call(
         first_edges, out_shape=(field, field, field, ints, fill, coef, slab2, slab2),
         in_specs=[vmem] * 9, out_specs=(vmem,) * 8,
-        input_output_aliases={3 + k: k for k in range(6)}, compiler_params=params, name="first_edges",
+        input_output_aliases={3 + k: k for k in range(6)}, scratch_shapes=[pltpu.VMEM(EXT[1:], F32)],
+        compiler_params=params, name="first_edges",
     )(row_c, row_d, tab, ex, hx, px, cx, fx, w)
     got2_a = swapped(send_a, "gx", 0)
     got2_b = swapped(send_b, "gx", 1)

time: 29.4 us -> 29 us (0.986)
  waiting for transfers between devices: 3.2 us -> 4.21 us
  Pallas kernels: 11.6 us -> 10.6 us
  starting transfers between devices: 13.5 us -> 13.2 us
    pallas_call x1 -> x0, Pallas kernels: 1.22 us -> none  [shards(): pl.pallas_call(near_coefs, out_shape=(field, field, field, ints, fill, co...]
    ppermute x6, waiting for transfers between devices: 3.2 us -> 4.21 us  [swapped(): return lax.ppermute(value, axis, pairs)]
    ppermute x6, starting transfers between devices: 13.5 us -> 13.2 us  [swapped(): return lax.ppermute(value, axis, pairs)]
  transfers between devices with their start and end apart: 6 -> 6, of which waited for: 1 -> 2; matrix products, arithmetic and copies ran while one was open for 0% -> 0% of each run, Pallas kernels for 27% -> 24%
where the time goes in v5:
time: 29 us; the launch traced here: 28.8 us
  starting transfers between devices  13.2 us (46%)
  Pallas kernels  10.6 us (37%)
  waiting for transfers between devices  4.21 us (15%)
  between operations  0.73 us (3%)
    ppermute x6, starting transfers between devices, swapped(): return lax.ppermute(value, axis, pairs)  13.2 us
    pallas_call x1, Pallas kernels, shards(): pl.pallas_call(interior, out_shape=shapes, in_specs=[hbm] * 6 + [vmem] *...  4.95 us
    ppermute x6, waiting for transfers between devices, swapped(): return lax.ppermute(value, axis, pairs)  4.21 us
    pallas_call x1, Pallas kernels, shards(): pl.pallas_call(load_and_pack, out_shape=(field, field, field, ints, fill,...  2.12 us
    pallas_call x1, Pallas kernels, shards(): pl.pallas_call(edge_b, out_shape=(result,) * 3 + shapes, in_specs=[vmem]...  1.68 us
    pallas_call x1, Pallas kernels, shards(): pl.pallas_call(edge_a, out_shape=shapes, in_specs=[vmem] * 8, out_specs=(...  0.96 us
    pallas_call x1, Pallas kernels, shards(): pl.pallas_call(first_edges, out_shape=(field, field, field, ints, fill, c...  0.74 us
  transfers between devices with their start and end apart: 6, of which 2 were waited for; matrix products, arithmetic and copies ran while one was open for 0% of the time, Pallas kernels for 24%

profile of v5, /device:TPU:130, one launch (start us, length us, event | category | flops | bytes accessed | tf_op | source)
XLA Modules:
  0.0 28.8 jit_solution(15622155235871494400)
XLA Ops:
  0.6 2.1 %load_and_pack.1 = (f32[3,21,56,128]{3,2,1,0:T(8,128)S(1)}, f32[3,21,56,128]{3,2,1,0:T(8,128)S(1)}, f32[3,21,56,128]{3,2,1,0:T(8,128)S(1)}, s32[2,21,56,128]{3,2...) custom-call(f32[3,16,32,128]{3,2,1,0:T(8,128)} %e.3, ...), custom_call_target="tpu_custom_call" | custom-call | tf_op jit(solution)/shard_map/load_and_pack/pallas_call | solution.py:522
  2.8 0.1 collective-permute-start
  2.9 2.5 %collective-permute-start.1 = (f32[6,16,8,128]{3,2,1,0:T(8,128)S(1)}, f32[6,16,8,128]{3,2,1,0:T(8,128)S(1)}, u32[]{:S(2)}, u32[]{:S(2)}) collective-permute-start(f32[6,16,8,128]{3,2,1,0:T(8,128)S(1)} %get-tuple-element.44), channel_id=1, source_target_pairs={{1,2},{2,1},{3,4},{4,3},{5,6},{6,5},{9,10},{10,9},{11,12},{12,11},... | collective-permute-start | bytes 1179656 | tf_op jit(solution)/shard_map/ppermute | solution.py:27
  5.4 1.7 %collective-permute-start.4 = (f32[15,32,128]{2,1,0:T(8,128)S(1)}, f32[15,32,128]{2,1,0:T(8,128)S(1)}, u32[]{:S(2)}, u32[]{:S(2)}) collective-permute-start(f32[15,32,128]{2,1,0:T(8,128)S(1)} %get-tuple-element.54), channel_id=1, source_target_pairs={{0,8},{8,0},{16,24},{24,16},{32,40},{40,32},{48,56},{56,48},{64,72... | collective-permute-start | bytes 737288 | tf_op jit(solution)/shard_map/ppermute | solution.py:27
  7.1 3.6 %collective-permute-start.5 = (f32[15,32,128]{2,1,0:T(8,128)S(1)}, f32[15,32,128]{2,1,0:T(8,128)S(1)}, u32[]{:S(2)}, u32[]{:S(2)}) collective-permute-start(f32[15,32,128]{2,1,0:T(8,128)S(1)} %get-tuple-element.55), channel_id=1, source_target_pairs={{8,16},{16,8},{24,32},{32,24},{40,48},{48,40},{56,64},{64,56},{72,... | collective-permute-start | bytes 737288 | tf_op jit(solution)/shard_map/ppermute | solution.py:27
  10.7 0.0 collective-permute-done.row_c
  10.7 1.3 %collective-permute-done.1.row_d = f32[6,16,8,128]{3,2,1,0:T(8,128)S(1)} collective-permute-done((f32[6,16,8,128]{3,2,1,0:T(8,128)S(1)}, f32[6,16,8,128]{3,2,1,0:T(8,128)S(1)}, u32[]{:S(2)}, u32[]{:S(2)}) %collective-permute-start.1) | collective-permute-done | bytes 393248 | tf_op jit(solution)/shard_map/ppermute | solution.py:27
  12.0 0.7 %first_edges.1 = (f32[3,21,56,128]{3,2,1,0:T(8,128)S(1)}, f32[3,21,56,128]{3,2,1,0:T(8,128)S(1)}, f32[3,21,56,128]{3,2,1,0:T(8,128)S(1)}, s32[2,21,56,128]{3,2,1...) custom-call(f32[6,16,8,128]{3,2,1,0:T(8,128)S(1)} %collective-permut, ...), custom_call_target="tpu_custom_call", output_to_operand_aliasing={{0}: (3, {}), {1}: (4, {}), {2}: (5, {}), {3}: (6, {}), {4}... | custom-call | tf_op jit(solution)/shard_map/first_edges/pallas_call | solution.py:532
  12.7 1.7 %collective-permute-start.3 = (f32[400,128]{1,0:T(8,128)S(1)}, f32[400,128]{1,0:T(8,128)S(1)}, u32[]{:S(2)}, u32[]{:S(2)}) collective-permute-start(f32[400,128]{1,0:T(8,128)S(1)} %get-tuple-element.53), channel_id=1, source_target_pairs={{0,8},{8,0},{16,24},{24,16},{32,40},{40,32},{48,56},{56,48},{64,72... | collective-permute-start | bytes 614408 | tf_op jit(solution)/shard_map/ppermute | solution.py:27
  14.4 3.6 %collective-permute-start.2 = (f32[400,128]{1,0:T(8,128)S(1)}, f32[400,128]{1,0:T(8,128)S(1)}, u32[]{:S(2)}, u32[]{:S(2)}) collective-permute-start(f32[400,128]{1,0:T(8,128)S(1)} %get-tuple-element.52), channel_id=1, source_target_pairs={{8,16},{16,8},{24,32},{32,24},{40,48},{48,40},{56,64},{64,56},{72,... | collective-permute-start | bytes 614408 | tf_op jit(solution)/shard_map/ppermute | solution.py:27
  18.0 5.0 %interior.1 = (f32[3,21,56,128]{3,2,1,0:T(8,128)S(1)}, f32[3,21,56,128]{3,2,1,0:T(8,128)S(1)}, f32[3,21,56,128]{3,2,1,0:T(8,128)S(1)}, s32[2,21,56,128]{3,2,1,0:...) custom-call(f32[3,16,32,128]{3,2,1,0:T(8,128)} %e.3, ...), custom_call_target="tpu_custom_call", output_to_operand_aliasing={{0}: (7, {}), {1}: (8, {}), {2}: (9, {}), {3}: (10, {}), {4... | custom-call | flops 80000000 | bytes 20000000 | tf_op jit(solution)/shard_map/interior/pallas_call | solution.py:542
  23.0 0.0 collective-permute-done.4.got1_a
  23.0 0.0 collective-permute-done.5.got1_b
  23.0 0.2 neighbour_cells.1
  23.1 0.0 collective-permute-done.3.got2
  23.2 1.0 %edge_a.1 = (f32[3,21,56,128]{3,2,1,0:T(8,128)S(1)}, f32[3,21,56,128]{3,2,1,0:T(8,128)S(1)}, f32[3,21,56,128]{3,2,1,0:T(8,128)S(1)}, s32[2,21,56,128]{3,2,1,0:T(...) custom-call(f32[400,128]{1,0:T(8,128)S(1)} %collective-permute-done., ...), custom_call_target="tpu_custom_call", output_to_operand_aliasing={{0}: (2, {}), {1}: (3, {}), {2}: (4, {}), {3}: (5, {}), {4}... | custom-call | tf_op jit(solution)/shard_map/edge_a/pallas_call | solution.py:552
  24.1 3.0 %collective-permute-done.2.got2 = f32[400,128]{1,0:T(8,128)S(1)} collective-permute-done((f32[400,128]{1,0:T(8,128)S(1)}, f32[400,128]{1,0:T(8,128)S(1)}, u32[]{:S(2)}, u32[]{:S(2)}) %collective-permute-start.2) | collective-permute-done | bytes 204832 | tf_op jit(solution)/shard_map/ppermute | solution.py:27
  27.1 1.7 %edge_b.1 = (f32[3,16,32,128]{3,2,1,0:T(8,128)}, f32[3,16,32,128]{3,2,1,0:T(8,128)}, f32[3,16,32,128]{3,2,1,0:T(8,128)}, f32[3,21,56,128]{3,2,1,0:T(8,128)S(1)},...) custom-call(f32[400,128]{1,0:T(8,128)S(1)} %collective-permute-done., ...), custom_call_target="tpu_custom_call", output_to_operand_aliasing={{3}: (2, {}), {4}: (3, {}), {5}: (4, {}), {6}: (5, {}), {7}... | custom-call | tf_op jit(solution)/shard_map/edge_b/pallas_call | solution.py:556
Async XLA Ops:
  2.8 7.9 %collective-permute-start = (f32[6,16,8,128]{3,2,1,0:T(8,128)S(1)}, f32[6,16,8,128]{3,2,1,0:T(8,128)S(1)}, u32[]{:S(2)}, u32[]{:S(2)}) collective-permute-start(f32[6,16,8,128]{3,2,1,0:T(8,128)S(1)} %get-tuple-element.43), channel_id=1, source_target_pairs={{0,1},{1,0},{2,3},{3,2},{4,5},{5,4},{6,7},{7,6},{8,9},{9,8},{10,11... | collective-permute-start | bytes 1179656 | tf_op jit(solution)/shard_map/ppermute | solution.py:27
  2.9 9.1 %collective-permute-start.1 = (f32[6,16,8,128]{3,2,1,0:T(8,128)S(1)}, f32[6,16,8,128]{3,2,1,0:T(8,128)S(1)}, u32[]{:S(2)}, u32[]{:S(2)}) collective-permute-start(f32[6,16,8,128]{3,2,1,0:T(8,128)S(1)} %get-tuple-element.44), channel_id=1, source_target_pairs={{1,2},{2,1},{3,4},{4,3},{5,6},{6,5},{9,10},{10,9},{11,12},{12,11},... | collective-permute-start | bytes 1179656 | tf_op jit(solution)/shard_map/ppermute | solution.py:27
  5.4 17.6 %collective-permute-start.4 = (f32[15,32,128]{2,1,0:T(8,128)S(1)}, f32[15,32,128]{2,1,0:T(8,128)S(1)}, u32[]{:S(2)}, u32[]{:S(2)}) collective-permute-start(f32[15,32,128]{2,1,0:T(8,128)S(1)} %get-tuple-element.54), channel_id=1, source_target_pairs={{0,8},{8,0},{16,24},{24,16},{32,40},{40,32},{48,56},{56,48},{64,72... | collective-permute-start | bytes 737288 | tf_op jit(solution)/shard_map/ppermute | solution.py:27
  7.1 15.9 %collective-permute-start.5 = (f32[15,32,128]{2,1,0:T(8,128)S(1)}, f32[15,32,128]{2,1,0:T(8,128)S(1)}, u32[]{:S(2)}, u32[]{:S(2)}) collective-permute-start(f32[15,32,128]{2,1,0:T(8,128)S(1)} %get-tuple-element.55), channel_id=1, source_target_pairs={{8,16},{16,8},{24,32},{32,24},{40,48},{48,40},{56,64},{64,56},{72,... | collective-permute-start | bytes 737288 | tf_op jit(solution)/shard_map/ppermute | solution.py:27
  12.7 10.4 %collective-permute-start.3 = (f32[400,128]{1,0:T(8,128)S(1)}, f32[400,128]{1,0:T(8,128)S(1)}, u32[]{:S(2)}, u32[]{:S(2)}) collective-permute-start(f32[400,128]{1,0:T(8,128)S(1)} %get-tuple-element.53), channel_id=1, source_target_pairs={{0,8},{8,0},{16,24},{24,16},{32,40},{40,32},{48,56},{56,48},{64,72... | collective-permute-start | bytes 614408 | tf_op jit(solution)/shard_map/ppermute | solution.py:27
  14.4 12.7 %collective-permute-start.2 = (f32[400,128]{1,0:T(8,128)S(1)}, f32[400,128]{1,0:T(8,128)S(1)}, u32[]{:S(2)}, u32[]{:S(2)}) collective-permute-start(f32[400,128]{1,0:T(8,128)S(1)} %get-tuple-element.52), channel_id=1, source_target_pairs={{8,16},{16,8},{24,32},{32,24},{40,48},{48,40},{56,64},{64,56},{72,... | collective-permute-start | bytes 614408 | tf_op jit(solution)/shard_map/ppermute | solution.py:27
